TPU v7x, 512 devices: a whole 4x8x8 slice. The times are simulated.
512 devices in a mesh: item: 8 (over y), rows: 32 (over z, x_hi, core), hid: 2 (over x_lo).
Axes of the slice: x: 4 (x_hi: 2, x_lo: 2; x = x_hi * 2 + x_lo), y: 8, z: 8, core: 2. Of those that a mesh axis runs over, the one named last changes fastest.
Arguments:
- latents: float32 [16, 32, 2048], P('item', 'rows'), may hold values from -6 to 6
- heights: int32 [16], P('item'), may hold values from 8 to 32, as said below
- widths: int32 [16], P('item'), may hold values from 8 to 32, as said below
- slot_item: int32 [16], P('item'), may hold values from 0 to 15, each once
- step_index: int32 [1], replicated, may hold values from 0 to 27
- cond_table: float32 [16, 5, 1536], replicated, may hold values from -9 to 9
- text_kv: bfloat16 [16, 2, 154, 768], P('item', None, None, 'hid'), may hold values from -175 to 175
- patch_weight: bfloat16 [64, 1536], replicated, may hold values from -0.75 to 0.75
- qkv_weight: bfloat16 [3, 1536, 768], P(None, ('item', 'rows'), 'hid'), may hold values from -0.15625 to 0.15625
- out_weight: bfloat16 [768, 1536], P('hid', ('item', 'rows')), may hold values from -0.21875 to 0.21875
- final_weight: bfloat16 [1536, 64], replicated, may hold values from -0.15625 to 0.15625
Outputs:
- next_latents: float32 [16, 32, 2048], P('item', 'rows')
- denoised: float32 [16, 32, 2048], P('item', 'rows')
Inputs may be any that keep to these rules, and one draw needn't show every extreme that they name: `heights`: every grid has at least 8 rows, and some item has exactly 32. `widths`: every grid has at least 8 columns, and some item has exactly 32. `slot_item`: each request is served by exactly one slot.
All inputs are finite; a program needn't handle non-finite values.
Results may differ from a plain program's by a relative error of at most 0.007.
Values may be sent and summed in bfloat16 or wider, within the bound.
A program may use at most 64 MiB of HBM per device.

v0:
```python
import jax
import jax.numpy as jnp
from jax import lax
from jax.sharding import PartitionSpec as P

HD = 64
STEPS = 28


def sigma_level(position):
    fraction = 1.0 - position / STEPS
    return 3.0 * fraction / (1.0 + 2.0 * fraction)


def position_embed(row_pos, col_count, model_width):
    quarter = model_width // 4
    frequency = 1.0 / 10000.0 ** (jnp.arange(quarter, dtype=jnp.float32) / quarter)
    col_pos = jnp.arange(col_count, dtype=jnp.float32)
    row_angle = row_pos[:, None] * frequency[None, :]
    col_angle = col_pos[:, None] * frequency[None, :]
    row_part = jnp.concatenate([jnp.sin(row_angle), jnp.cos(row_angle)], 1)
    col_part = jnp.concatenate([jnp.sin(col_angle), jnp.cos(col_angle)], 1)
    row_full = jnp.broadcast_to(
        row_part[:, None, :], (row_pos.shape[0], col_count, model_width // 2)
    )
    col_full = col_part[None, :, :]
    return jnp.concatenate([row_full, col_full], 2)


def normalize(values):
    mean_rows = jnp.mean(values, -1, keepdims=True)
    centered = values - mean_rows
    return centered * lax.rsqrt(jnp.mean(centered * centered, -1, keepdims=True) + 1e-06)


def body(
    latents,
    heights,
    widths,
    slot_item,
    step_index,
    cond_table,
    text_kv,
    patch_weight,
    qkv_weight,
    out_weight,
    final_weight,
):
    slot_count = latents.shape[0]
    rows_here = latents.shape[1]
    channels = patch_weight.shape[0]
    model_width = patch_weight.shape[1]
    col_count = latents.shape[2] // channels
    local_width = text_kv.shape[3]
    heads_here = local_width // HD
    text_count = text_kv.shape[2]
    per_slot = rows_here * col_count
    tok_rows = slot_count * per_slot
    row_start = lax.axis_index("rows") * rows_here
    row_pos = (row_start + jnp.arange(rows_here, dtype=jnp.int32)).astype(jnp.float32)
    patches = latents.reshape(tok_rows, channels).astype(jnp.bfloat16)
    embedded = jnp.dot(patches, patch_weight, preferred_element_type=jnp.float32).reshape(
        slot_count, per_slot, model_width
    )
    embedded = embedded + position_embed(row_pos, col_count, model_width)
    entries = cond_table.shape[0]
    chosen = (slot_item[:, None] == jnp.arange(entries, dtype=jnp.int32)[None, :]).astype(
        jnp.float32
    )
    conditions = jnp.dot(
        chosen, cond_table.reshape(entries, 5 * model_width), precision=lax.Precision.HIGHEST
    )
    conditions = conditions.reshape(slot_count, 5, model_width)
    normed = (normalize(embedded) * (1.0 + conditions[:, 1:2, :]) + conditions[:, 0:1, :]).astype(
        jnp.bfloat16
    )
    flat_rows = normed.reshape(tok_rows, model_width)
    projected = jnp.einsum(
        "td,kdh->kth",
        flat_rows,
        lax.all_gather(qkv_weight, ("item", "rows"), axis=1, tiled=True),
        preferred_element_type=jnp.float32,
    )
    projected = projected.astype(jnp.bfloat16)
    queries = projected[0].reshape(slot_count, per_slot, heads_here, HD)
    image_kv = projected[1:].reshape(2, slot_count, rows_here, col_count, local_width)
    score_scale = HD ** (-0.5)
    text_keys = text_kv[:, 0].reshape(slot_count, text_count, heads_here, HD)
    text_vals = text_kv[:, 1].reshape(slot_count, text_count, heads_here, HD)
    text_score = (
        jnp.einsum("sqhd,skhd->shqk", queries, text_keys, preferred_element_type=jnp.float32)
        * score_scale
    )
    first_top = jnp.max(text_score, -1)
    text_weights = jnp.exp(text_score - first_top[..., None])
    first_total = jnp.sum(text_weights, -1)
    first_acc = jnp.einsum(
        "shqk,skhd->shqd",
        text_weights.astype(jnp.bfloat16),
        text_vals,
        preferred_element_type=jnp.float32,
    )
    col_live = jnp.arange(col_count, dtype=jnp.int32)[None, :] < widths[:, None]
    gathered = lax.all_gather(image_kv, "rows", axis=2, tiled=True)
    run_top = first_top
    run_total = first_total
    run_acc = first_acc
    key_rows = gathered.shape[2]
    key_piece = gathered[0].reshape(slot_count, key_rows * col_count, heads_here, HD)
    val_piece = gathered[1].reshape(slot_count, key_rows * col_count, heads_here, HD)
    scores = (
        jnp.einsum("sqhd,skhd->shqk", queries, key_piece, preferred_element_type=jnp.float32)
        * score_scale
    )
    key_index = jnp.arange(key_rows, dtype=jnp.int32)
    live_mask = (key_index[None, :, None] < heights[:, None, None]) & col_live[:, None, :]
    live_mask = live_mask.reshape(slot_count, 1, 1, key_rows * col_count)
    scores = jnp.where(live_mask, scores, -1e30)
    new_top = jnp.maximum(run_top, jnp.max(scores, -1))
    factor = jnp.exp(run_top - new_top)
    weights = jnp.exp(scores - new_top[..., None])
    run_total = run_total * factor + jnp.sum(weights, -1)
    run_acc = run_acc * factor[..., None] + jnp.einsum(
        "shqk,skhd->shqd",
        weights.astype(jnp.bfloat16),
        val_piece,
        preferred_element_type=jnp.float32,
    )
    run_top, run_total, run_acc = (new_top, run_total, run_acc)
    attended = (
        (run_acc / run_total[..., None])
        .transpose(0, 2, 1, 3)
        .reshape(tok_rows, local_width)
        .astype(jnp.bfloat16)
    )
    partial_value = jnp.dot(
        attended,
        lax.all_gather(out_weight, ("item", "rows"), axis=1, tiled=True),
        preferred_element_type=jnp.float32,
    )
    summed = lax.psum(partial_value.astype(jnp.bfloat16), "hid").astype(jnp.float32)
    summed = summed.reshape(slot_count, per_slot, model_width)
    residual = embedded + conditions[:, 2:3, :] * summed
    final_in = (normalize(residual) * (1.0 + conditions[:, 4:5, :]) + conditions[:, 3:4, :]).astype(
        jnp.bfloat16
    )
    velocity = jnp.dot(
        final_in.reshape(tok_rows, model_width), final_weight, preferred_element_type=jnp.float32
    )
    position = step_index[0].astype(jnp.float32)
    sigma_now = sigma_level(position)
    sigma_next = sigma_level(position + 1.0)
    row_global = row_start + jnp.arange(rows_here, dtype=jnp.int32)
    live_patch = (row_global[None, :, None] < heights[:, None, None]) & col_live[:, None, :]
    velocity = velocity.reshape(slot_count, rows_here, col_count, channels)
    live_velocity = jnp.where(live_patch[..., None], velocity, 0.0).reshape(
        slot_count, rows_here, col_count * channels
    )
    next_latents = latents + (sigma_next - sigma_now) * live_velocity
    denoised = latents - sigma_now * live_velocity
    return (next_latents, denoised)


def solution(mesh):
    return jax.shard_map(
        body,
        mesh=mesh,
        in_specs=(
            P("item", "rows", None),
            P("item"),
            P("item"),
            P("item"),
            P(),
            P(),
            P("item", None, None, "hid"),
            P(),
            P(None, ("item", "rows"), "hid"),
            P("hid", ("item", "rows")),
            P(),
        ),
        out_specs=(P("item", "rows", None), P("item", "rows", None)),
        check_vma=False,
    )
```

profile of v0, /device:TPU:1, one launch (start us, length us, event | category | flops | bytes accessed | tf_op | source)
XLA Modules:
  0.0 422.9 jit_solution(1402297968687768749)
XLA Ops:
  7.2 0.0 all-gather.5.cloned.1.call-start
  7.2 1.4 copy.35
  8.6 0.0 all-gather.5.cloned.1.call-update
  8.6 0.0 all-gather.9.cloned.1.call-start
  8.7 0.7 all-gather.9.cloned.1.call-update
  9.4 0.0 all-gather.7.cloned.1.call-start
  9.5 0.1 fusion.49
  9.5 0.2 fusion.42
  9.8 0.8 convert_reduce_fusion
  10.6 0.1 convert_element_type.46
  10.7 1.2 fusion.56
  11.9 0.2 multiply_reduce_fusion.1
  12.1 0.3 fusion.25
  12.4 0.1 add_convert_fusion.1
  12.6 136.8 %all-gather.5.cloned.1.call-done = bf16[3,1536,384]{2,0,1:T(4,128)(2,1)} async-done(((bf16[3,6,384]{2,0,1:T(4,128)(2,1)}), bf16[3,1536,384]{2,0,1:T(4,128)(2,1)}) %all-gather.5.cloned.1.call-update) | async-done | bytes 3538960 | tf_op jit(solution)/shard_map/all_gather | solution.py:81
  149.4 3.1 fusion.20
  152.5 0.6 slice.48
  153.1 0.0 all-gather.7.cloned.1.call-update
  153.2 0.0 all-reduce.2.cloned.1.call-start
  153.2 0.1 broadcast_and_fusion.1
  153.3 0.1 broadcast_and_fusion
  153.4 0.1 and.40
  153.5 0.7 fusion.54
  154.2 0.5 copy.37
  154.7 0.5 copy.39
  155.2 109.8 %all-gather.9.cloned.1.call-done = bf16[256,6,384]{2,1,0:T(8,128)(2,1)} async-done(((bf16[1,6,384]{2,1,0:T(8,128)(2,1)}), bf16[256,6,384]{2,1,0:T(8,128)(2,1)}) %all-gather.9.cloned.1.call-update) | async-done | bytes 1179664 | tf_op jit(solution)/shard_map/all_gather | solution.py:138
  265.0 3.3 reshape.279
  268.3 0.1 reshape_squeeze.15
  268.4 0.3 fusion.57
  268.7 0.2 fusion.28
  268.9 85.4 %all-gather.7.cloned.1.call-done = bf16[2,2,32,32,384]{4,3,2,1,0:T(8,128)(2,1)} async-done(((bf16[2,2,1,32,384]{4,3,2,1,0:T(8,128)(2,1)}), bf16[2,2,32,32,384]{4,3,2,1,0:T(8,128)(2,1)}) %all-gather.7.cloned.1.call-update) | async-done | bytes 3145744 | tf_op jit(solution)/shard_map/all_gather | solution.py:104
  354.4 3.5 fusion.53
  357.8 3.7 reshape_squeeze.18
  361.6 3.4 fusion.58
  365.0 5.9 %reshape_squeeze.19 = bf16[2,1024,6,64]{3,2,1,0:T(8,128)(2,1)} reshape(bf16[1,2,32,32,384]{4,3,2,1,0:T(8,128)(2,1)} %get-tuple-element.5) | data formatting | bytes 3145728 | tf_op jit(solution)/shard_map/reshape;squeeze | solution.py:110
  370.9 0.4 fusion.8
  371.3 3.3 fusion.16
  374.6 0.3 fusion.19
  375.0 0.1 convert_element_type.54
  375.1 0.7 copy-done.1
  375.9 1.2 convolution_convert_fusion
  377.8 34.3 %all-reduce.2.cloned.1.call-done = bf16[2,32,1536]{2,1,0:T(8,128)(2,1)} async-done(((bf16[2,32,1536]{2,1,0:T(8,128)(2,1)}), bf16[2,32,1536]{2,1,0:T(8,128)(2,1)}) %all-reduce.2.cloned.1.call-update) | async-done | bytes 196624 | tf_op jit(solution)/shard_map/psum | solution.py:141
  412.1 1.1 fusion.38
  413.2 1.1 multiply_reduce_fusion
  414.3 1.2 broadcast_multiply_fusion
  415.5 0.1 mul.213
  415.6 0.1 mul.214
  415.7 0.6 fusion.55
  (31 shorter events, 0.2 us)
Async XLA Ops:
  7.2 4.9 %copy-start = (f32[16,5,1536]{2,0,1:T(8,128)S(1)}, f32[16,5,1536]{2,0,1:T(8,128)}, u32[]{:S(2)}) copy-start(f32[16,5,1536]{2,0,1:T(8,128)} %param.16) | copy-start | bytes 1474564
  7.2 4.9 %copy-start.4 = (s32[2]{0:T(128)S(1)}, s32[2]{0:T(128)}, u32[]{:S(2)}) copy-start(s32[2]{0:T(128)} %param.14) | copy-start | bytes 28
  7.2 142.2 %all-gather.5.cloned.1.call-start = ((), (), s32[]{:S(2)}) async-start(), calls=%async_computation | async-start | bytes 4737024 | tf_op jit(solution)/shard_map/all_gather | solution.py:81
  8.6 256.3 %all-gather.9.cloned.1.call-start = ((), (), s32[]{:S(2)}) async-start(), calls=%async_computation.3 | async-start | bytes 1579008 | tf_op jit(solution)/shard_map/all_gather | solution.py:138
  9.4 345.0 %all-gather.7.cloned.1.call-start = ((), (), s32[]{:S(2)}) async-start(), calls=%async_computation.1 | async-start | bytes 3244032 | tf_op jit(solution)/shard_map/all_gather | solution.py:104
  149.4 3.9 copy-start.5
  149.4 3.9 copy-start.6
  149.4 4.1 copy-start.2
  153.2 258.9 %all-reduce.2.cloned.1.call-start = ((), (), s32[]{:S(2)}) async-start(), calls=%async_computation.2 | async-start | bytes 393216 | tf_op jit(solution)/shard_map/psum | solution.py:141
  374.6 1.3 copy-start.1
  375.0 39.3 %copy-start.7 = (bf16[1536,64]{0,1:T(8,128)(2,1)S(1)}, bf16[1536,64]{0,1:T(8,128)(2,1)}, u32[]{:S(2)}) copy-start(bf16[1536,64]{0,1:T(8,128)(2,1)} %param.21) | copy-start | bytes 589828
  377.0 38.7 %copy-start.3 = (f32[2,1,2048]{2,1,0:T(1,128)S(1)}, f32[2,1,2048]{2,1,0:T(1,128)}, u32[]{:S(2)}) copy-start(f32[2,1,2048]{2,1,0:T(1,128)} %param.11) | copy-start | bytes 49156
Sparse Core Ops, SparseCore 0:
  12.5 136.7 all-gather.4
  153.5 111.3 all-gather.8
  268.3 86.0 all-gather.6
  377.2 34.8 all-reduce.1
where the time goes:
time: 423 us
  waiting for transfers between devices  367 us (87%)
  local copies, waits for them, and re-layouts  21.5 us (5%)
  between operations  14.8 us (3%)
  matrix products  14.3 us (3%)
  other arithmetic  5.08 us (1%)
    all_gather x1, waiting for transfers between devices, body(): lax.all_gather(qkv_weight, ('item', 'rows'), axis=1, tiled=True)  137 us
    all_gather x1, waiting for transfers between devices, body(): lax.all_gather(out_weight, ('item', 'rows'), axis=1, tiled=True)  110 us
    all_gather x1, waiting for transfers between devices, body(): gathered = lax.all_gather(image_kv, 'rows', axis=2, tiled=True)  85.4 us
    psum x1, waiting for transfers between devices, body(): lax.psum(partial_value.astype(jnp.bfloat16), 'hid').astype(jnp.float32)  34.3 us
  transfers between devices with their start and end apart: 4, of which 4 were waited for; matrix products, arithmetic and copies ran while one was open for 3% of the time, Pallas kernels for 0%

commit v1 on v0

v1 whole, which is shorter than its diff:
```python
import functools

import jax
import jax.numpy as jnp
import numpy as np
from jax import lax
from jax.experimental import pallas as pl
from jax.experimental.pallas import tpu as pltpu
from jax.sharding import PartitionSpec as P

MESH = pl.DeviceIdType.MESH
HD = 64
STEPS = 28
D = 1536
NY, NZ = 8, 8
UR = 96
F32, BF16 = jnp.float32, jnp.bfloat16


def feature_order():
    order = np.zeros((D,), np.int32)
    at = 0
    for core in range(2):
        for outer in range(8):
            for inner in range(8):
                y, z = (outer, inner) if core == 0 else (inner, outer)
                for xh in range(2):
                    block = y * 32 + z * 4 + xh * 2 + core
                    order[at : at + 6] = 6 * block + np.arange(6)
                    at += 6
    return order


def tables():
    order = feature_order()
    quarter = D // 4
    frequency = (
        np.float32(1.0) / np.float32(10000.0) ** (np.arange(quarter, dtype=np.float32) / np.float32(quarter))
    ).astype(np.float32)
    angle = np.arange(32, dtype=np.float32)[:, None] * frequency[None, :]
    part = np.concatenate([np.sin(angle.astype(np.float64)), np.cos(angle.astype(np.float64))], 1)
    zero = np.zeros_like(part)
    row_table = np.concatenate([part, zero], 1)[:, order].astype(np.float32)
    col_table = np.concatenate([zero, part], 1)[:, order].astype(np.float32)
    pick = np.zeros((480, 1), np.int32)
    for tile in range(5):
        for source in range(16):
            for j in range(6):
                pick[tile * 96 + source * 6 + j, 0] = source * 32 + tile * 6 + j
    col_table = np.stack([col_table[0::2], col_table[1::2]])
    return order[None, :], pick, row_table[:, None, :], col_table


def relative_partners():
    found = set()
    for dy in range(NY):
        for dz in range(NZ):
            for dxh in range(2):
                for dc in range(2):
                    for dxl in range(2):
                        near = (dy == 0 and dxl == 0) or (dy == 0 and dz == 0)
                        near = near or (dc == 0 and (dy == 0 or dz == 0))
                        if near:
                            found.add((dy, dz, dxh, dc, dxl))
    found.discard((0, 0, 0, 0, 0))
    return sorted(found)


def kernel(
    heights,
    widths,
    slot_item,
    step_index,
    lat,
    latb,
    cond,
    text,
    wp,
    wft,
    qpiece,
    opiece,
    order,
    pick,
    rowtab,
    coltab,
    next_out,
    den_out,
    lb,
    qb,
    ob,
    qu,
    ou,
    nb,
    kvb,
    wps,
    wfs,
    cperm,
    rows_in,
    rows_out,
    eb,
    send_att,
    recv_att,
    sem_ls,
    sem_lr,
    sem_qs,
    sem_qr,
    sem_os,
    sem_or,
    sem_us,
    sem_ur,
    sem_ps,
    sem_pr,
    sem_ws,
    sem_wr,
    sem_xs,
    sem_xr,
    sem_as,
    sem_ar,
):
    y = lax.axis_index("item")
    rows = lax.axis_index("rows")
    xl = lax.axis_index("hid")
    z = rows // 4
    xh = (rows // 2) % 2
    core = rows % 2
    by_b = z * (1 - core) + y * core
    by_c = y * (1 - core) + z * core

    def flip(bit, change):
        return bit if change == 0 else 1 - bit

    def device(ty, tz, txh, tc, txl):
        return (ty, tz * 4 + txh * 2 + tc, txl)

    def ring_b(k):
        return (y + core * k) % 8, (z + (1 - core) * k) % 8

    def ring_c(k):
        return (y + (1 - core) * k) % 8, (z + core * k) % 8

    barrier = pltpu.get_barrier_semaphore()
    partners = relative_partners()
    for dy, dz, dxh, dc, dxl in partners:
        pl.semaphore_signal(
            barrier,
            inc=1,
            device_id=device((y + dy) % 8, (z + dz) % 8, flip(xh, dxh), flip(core, dc), flip(xl, dxl)),
            device_id_type=MESH,
        )
    lb[rows] = latb[core]
    qb[by_b * 2 + xh] = qpiece[xh]
    ob[xl * 16 + by_b * 2 + xh] = opiece[...]
    pl.semaphore_wait(barrier, len(partners))

    def remote(src, dst, s_sem, r_sem, to):
        return pltpu.make_async_remote_copy(
            src_ref=src, dst_ref=dst, send_sem=s_sem, recv_sem=r_sem, device_id=to, device_id_type=MESH
        )

    q_copies, l_copies, o_copies = [], [], []
    for k in range(8):
        for dxh in range(2):
            if k == 0 and dxh == 0:
                continue
            ty, tz = ring_b(k)
            txh = flip(xh, dxh)
            n = k * 2 + dxh
            q_copies.append(
                remote(
                    qpiece.at[txh],
                    qb.at[by_b * 2 + xh],
                    sem_qs.at[n],
                    sem_qr.at[n],
                    device(ty, tz, txh, core, xl),
                )
            )
            q_copies[-1].start()
    for dz in range(8):
        for dxh in range(2):
            for dc in range(2):
                n = dz * 4 + dxh * 2 + dc
                if n == 0:
                    continue
                tc = flip(core, dc)
                l_copies.append(
                    remote(
                        latb.at[tc],
                        lb.at[rows],
                        sem_ls.at[n],
                        sem_lr.at[n],
                        device(y, (z + dz) % 8, flip(xh, dxh), tc, xl),
                    )
                )
                l_copies[-1].start()
    for k in range(8):
        for dxh in range(2):
            for dxl in range(2):
                n = k * 4 + dxh * 2 + dxl
                if n == 0:
                    continue
                ty, tz = ring_b(k)
                o_copies.append(
                    remote(
                        opiece,
                        ob.at[xl * 16 + by_b * 2 + xh],
                        sem_os.at[n],
                        sem_or.at[n],
                        device(ty, tz, flip(xh, dxh), core, flip(xl, dxl)),
                    )
                )
                o_copies[-1].start()

    eb[...] = (lax.broadcasted_iota(jnp.int32, (480, 512), 1) == pick[...]).astype(F32).astype(BF16)
    rows_in[0:64] = wp[...]
    rows_in[64:128] = wft[...]
    for s in range(2):
        c = cond[slot_item[s]]
        hi = c.astype(BF16)
        mid = (c - hi.astype(F32)).astype(BF16)
        low = (c - hi.astype(F32) - mid.astype(F32)).astype(BF16)
        zero = jnp.zeros((3, D), F32)
        for i, piece in enumerate((hi, mid, low)):
            at = 128 + s * 24 + i * 8
            cperm[at - 128 : at - 120] = jnp.concatenate([piece.astype(F32), zero], 0)
    rows_in[128:176] = cperm[0:48].astype(BF16)
    for i in range(6):
        cols = slice(i * 256, (i + 1) * 256)
        onehot = (
            (lax.broadcasted_iota(jnp.int32, (D, 256), 0) == order[:, cols]).astype(F32).astype(BF16)
        )
        rows_out[:, cols] = jnp.dot(rows_in[...], onehot, preferred_element_type=F32)
    blank = jnp.zeros((64, D), BF16)
    wps[0, 0:64] = rows_out[0:64].astype(BF16)
    wps[0, 64:128] = blank
    wps[1, 0:64] = blank
    wps[1, 64:128] = rows_out[0:64].astype(BF16)
    wfs[0, 0:64] = rows_out[64:128].astype(BF16)
    wfs[0, 64:128] = blank
    wfs[1, 0:64] = blank
    wfs[1, 64:128] = rows_out[64:128].astype(BF16)
    for s in range(2):
        at = 128 + s * 24
        cperm[s * 8 : s * 8 + 8] = (
            rows_out[at : at + 8] + rows_out[at + 8 : at + 16] + rows_out[at + 16 : at + 24]
        )

    for copy in q_copies:
        copy.wait_recv()
    packed = jnp.dot(eb[...], qb[...].reshape(512, 128), preferred_element_type=F32).astype(BF16)
    mine = core * 8 + by_c
    for t in range(5):
        qu[mine, :, t * 128 : (t + 1) * 128] = packed[t * 96 : (t + 1) * 96]

    def unit(step):
        return core * 8 + (by_c + step + 8) % 8

    class Spread:
        def __init__(self, buf, s_sem, r_sem, ps_sem, pr_sem):
            self.buf, self.s, self.r, self.ps, self.pr = buf, s_sem, r_sem, ps_sem, pr_sem
            self.sent, self.come = [], {}
            self.partner = []

        def send(self, n, origin, step):
            ty, tz = ring_c((step + 8) % 8)
            slot = unit(origin)
            c = remote(
                self.buf.at[slot],
                self.buf.at[slot],
                self.s.at[n],
                self.r.at[n],
                device(ty, tz, xh, core, xl),
            )
            c.start()
            self.sent.append(c)
            self.come[n] = c

        def share(self, n, origin):
            slot = unit(origin)
            c = remote(
                self.buf.at[slot],
                self.buf.at[slot],
                self.ps.at[n],
                self.pr.at[n],
                device(y, z, xh, 1 - core, xl),
            )
            c.start()
            self.partner.append(c)

        def first(self):
            self.send(0, 0, 2)
            self.send(1, 0, -2)
            self.send(2, 0, 1)
            self.send(3, 0, -1)
            self.share(0, 0)

        def second(self):
            self.come[0].wait_recv()
            self.send(4, -2, 1)
            self.send(6, -2, 2)
            self.come[1].wait_recv()
            self.send(5, 2, -1)
            self.share(1, -2)
            self.share(2, 2)
            self.come[2].wait_recv()
            self.share(3, -1)
            self.come[3].wait_recv()
            self.share(4, 1)

        def third(self):
            self.come[4].wait_recv()
            self.share(5, -3)
            self.come[5].wait_recv()
            self.share(6, 3)
            self.come[6].wait_recv()
            self.share(7, -4)

        def last(self):
            for c in self.partner:
                c.wait_recv()

        def close(self):
            for c in self.sent + self.partner:
                c.wait_send()

    qs = Spread(qu, sem_us, sem_ur, sem_ps, sem_pr)
    qs.first()

    def normalise(value):
        mean = jnp.mean(value, -1, keepdims=True)
        centered = value - mean
        return centered * lax.rsqrt(jnp.mean(centered * centered, -1, keepdims=True) + 1e-06)

    for copy in l_copies:
        copy.wait_recv()

    cmine = cperm[pl.ds(pl.multiple_of(core * 8, 8), 8)]
    shift_a, scale_a = cmine[0:1], 1.0 + cmine[1:2]

    def norm_chunk(i, carry):
        x = lb[pl.ds(i * 4, 4)].reshape(64, 128)
        for parity in range(2):
            e = jnp.dot(x, wps[parity], preferred_element_type=F32)
            for rr in range(4):
                part = e[rr * 16 : rr * 16 + 16] + (rowtab[i * 4 + rr] + coltab[parity])
                at = pl.multiple_of(i * 128 + parity * 64 + rr * 16, 16)
                nb[pl.ds(at, 16)] = (normalise(part) * scale_a + shift_a).astype(BF16)
        return carry

    lax.fori_loop(0, 4, norm_chunk, 0)
    qs.second()
    for copy in o_copies:
        copy.wait_recv()
    for half in range(2):
        got = jnp.dot(
            eb[0:288], ob[half * 16 : half * 16 + 16].reshape(512, 128), preferred_element_type=F32
        ).astype(BF16)
        for t in range(3):
            ou[mine, :, half * 384 + t * 128 : half * 384 + (t + 1) * 128] = got[t * 96 : (t + 1) * 96]
    lax.fori_loop(4, 8, norm_chunk, 0)
    ws = Spread(ou, sem_ws, sem_wr, sem_xs, sem_xr)
    ws.first()
    qs.third()
    qs.last()

    def kv_chunk(i, carry):
        at = pl.ds(pl.multiple_of(i * 256, 256), 256)
        weight = qu[:, :, 0:384].reshape(D, 384)
        kvb[at] = jnp.dot(nb[at], weight, preferred_element_type=F32).astype(BF16)
        return carry

    lax.fori_loop(0, 4, kv_chunk, 0)
    queries = jnp.dot(
        nb[pl.ds(pl.multiple_of(z * 128, 128), 128)],
        qu[:, :, 384:640].reshape(D, 256),
        preferred_element_type=F32,
    ).astype(BF16)
    queries = jnp.concatenate([queries, jnp.zeros((128, 128), BF16)], 1)
    ws.second()

    r_id = lax.broadcasted_iota(jnp.int32, (384, 384), 0)
    c_id = lax.broadcasted_iota(jnp.int32, (384, 384), 1)
    pick_key = ((r_id == c_id + 192 * xh) & (c_id < 192)).astype(F32).astype(BF16)
    pick_val = ((r_id == c_id - 192 + 192 * xh) & (c_id >= 192)).astype(F32).astype(BF16)
    place = ((r_id - 192 + 192 * xh == c_id) & (r_id >= 192)).astype(F32).astype(BF16)
    text_rows = (
        jnp.dot(text[core, 0], pick_key, preferred_element_type=F32)
        + jnp.dot(text[core, 1], pick_val, preferred_element_type=F32)
    ).astype(BF16)

    height, width = heights[core], widths[core]
    key_id = lax.broadcasted_iota(jnp.int32, (1, 1024), 1)
    key_row = (key_id // 128) * 4 + (key_id // 16) % 4
    key_col = (key_id % 16) * 2 + (key_id // 64) % 2
    live = (key_row < height) & (key_col < width)
    lane = lax.broadcasted_iota(jnp.int32, (1, 384), 1)
    nt = (((1,), (1,)), ((), ()))
    kv = kvb[...]
    attended = jnp.zeros((128, 384), F32)
    for h in range(3):
        q_h = jnp.where((lane >= 64 * h) & (lane < 64 * h + 64), queries.astype(F32), 0.0).astype(BF16)
        s_text = lax.dot_general(q_h, text_rows, nt, preferred_element_type=F32) * HD ** (-0.5)
        s_img = lax.dot_general(q_h, kv, nt, preferred_element_type=F32) * HD ** (-0.5)
        s_img = jnp.where(live, s_img, -1e30)
        top = jnp.maximum(jnp.max(s_text, -1, keepdims=True), jnp.max(s_img, -1, keepdims=True))
        w_text = jnp.exp(s_text - top)
        w_img = jnp.exp(s_img - top)
        total = jnp.sum(w_text, -1, keepdims=True) + jnp.sum(w_img, -1, keepdims=True)
        acc = jnp.dot(w_text.astype(BF16), text_rows, preferred_element_type=F32) + jnp.dot(
            w_img.astype(BF16), kv, preferred_element_type=F32
        )
        inside = (lane >= 192 + 64 * h) & (lane < 256 + 64 * h)
        attended = attended + jnp.where(inside, acc / total, 0.0)
    placed = jnp.dot(attended.astype(BF16), place, preferred_element_type=F32).astype(BF16)
    for j in range(4):
        for parity in range(2):
            send_att[j, parity * 16 : parity * 16 + 16] = placed[
                parity * 64 + j * 16 : parity * 64 + j * 16 + 16
            ]
    head_at = xl * 2 + xh
    a_copies = []
    for n in range(1, 8):
        txh, tc, txl = flip(xh, n // 4), flip(core, (n // 2) % 2), flip(xl, n % 2)
        a_copies.append(
            remote(
                send_att.at[txh * 2 + tc],
                recv_att.at[core, head_at],
                sem_as.at[n],
                sem_ar.at[n],
                device(y, z, txh, tc, txl),
            )
        )
        a_copies[-1].start()
    recv_att[core, head_at] = send_att[xh * 2 + core]
    ws.third()
    ws.last()
    for copy in a_copies:
        copy.wait_recv()

    step = jnp.zeros((1, 128), F32) + step_index[0].astype(F32)

    def sigma_level(position):
        fraction = 1.0 - position / STEPS
        return 3.0 * fraction / (1.0 + 2.0 * fraction)

    sigma_now = sigma_level(step)
    sigma_next = sigma_level(step + 1.0)

    halves = [
        jnp.concatenate([recv_att[s, 2 * g] + recv_att[s, 2 * g + 1] for s in range(2)], 0) for g in range(2)
    ]
    projected = lax.dot_general(
        jnp.concatenate(halves, 1), ou[...].reshape(D, 768), nt, preferred_element_type=F32
    )
    for s in range(2):
        gate = cperm[s * 8 + 2 : s * 8 + 3]
        shift_f = cperm[s * 8 + 3 : s * 8 + 4]
        scale_f = 1.0 + cperm[s * 8 + 4 : s * 8 + 5]
        velocity = jnp.zeros((16, 128), F32)
        for parity in range(2):
            e = jnp.dot(latb[s], wps[parity], preferred_element_type=F32) + (rowtab[rows] + coltab[parity])
            at = s * 32 + parity * 16
            residual = e + gate * projected[at : at + 16]
            final_in = (normalise(residual) * scale_f + shift_f).astype(BF16)
            velocity = velocity + lax.dot_general(final_in, wfs[parity], nt, preferred_element_type=F32)
        m_id = lax.broadcasted_iota(jnp.int32, (16, 128), 0)
        l_id = lax.broadcasted_iota(jnp.int32, (16, 128), 1)
        row_live = jnp.where(rows < heights[s], 1, 0)
        alive = (m_id * 2 + l_id // 64 < widths[s] * row_live)
        velocity = jnp.where(alive, velocity, 0.0)
        next_out[s] = lat[s] + (sigma_next - sigma_now) * velocity
        den_out[s] = lat[s] - sigma_now * velocity

    for copy in q_copies + l_copies + o_copies + a_copies:
        copy.wait_send()
    qs.close()
    ws.close()


def body(
    latents,
    heights,
    widths,
    slot_item,
    step_index,
    cond_table,
    text_kv,
    patch_weight,
    qkv_weight,
    out_weight,
    final_weight,
):
    order, pick, rowtab, coltab = tables()
    lat = latents.reshape(2, 16, 128)
    latb = lat.astype(BF16)
    w = jnp.stack([qkv_weight[1], qkv_weight[2], qkv_weight[0]])
    w = w.reshape(3, 6, 2, 192).transpose(2, 1, 0, 3).reshape(2, 6, 576)
    w = jnp.pad(w, ((0, 0), (0, 0), (0, 64))).reshape(2, 6, 5, 128).transpose(0, 2, 1, 3)
    qpiece = jnp.pad(w.reshape(2, 30, 128), ((0, 0), (0, 2), (0, 0)))
    o = out_weight.T.reshape(6, 3, 128).transpose(1, 0, 2).reshape(18, 128)
    opiece = jnp.pad(o, ((0, 14), (0, 0)))
    smem = pl.BlockSpec(memory_space=pltpu.SMEM)
    vmem = pl.BlockSpec(memory_space=pltpu.VMEM)
    dma = pltpu.SemaphoreType.DMA
    shape = jax.ShapeDtypeStruct((2, 16, 128), F32)
    outs = pl.pallas_call(
        kernel,
        out_shape=(shape, shape),
        in_specs=[smem] * 4 + [vmem] * 12,
        out_specs=(vmem, vmem),
        scratch_shapes=[
            pltpu.VMEM((32, 16, 128), BF16),
            pltpu.VMEM((16, 32, 128), BF16),
            pltpu.VMEM((32, 32, 128), BF16),
            pltpu.VMEM((16, UR, 640), BF16),
            pltpu.VMEM((16, UR, 768), BF16),
            pltpu.VMEM((1024, D), BF16),
            pltpu.VMEM((1024, 384), BF16),
            pltpu.VMEM((2, 128, D), BF16),
            pltpu.VMEM((2, 128, D), BF16),
            pltpu.VMEM((48, D), F32),
            pltpu.VMEM((176, D), BF16),
            pltpu.VMEM((176, D), F32),
            pltpu.VMEM((480, 512), BF16),
            pltpu.VMEM((4, 32, 384), BF16),
            pltpu.VMEM((2, 4, 32, 384), BF16),
        ]
        + [dma((n,)) for n in (32, 32, 16, 16, 32, 32, 7, 7, 8, 8, 7, 7, 8, 8, 8, 8)],
        compiler_params=pltpu.CompilerParams(
            collective_id=0, has_side_effects=True, vmem_limit_bytes=56 * 1024 * 1024
        ),
    )(
        heights,
        widths,
        slot_item,
        step_index,
        lat,
        latb,
        cond_table,
        text_kv,
        patch_weight,
        final_weight.T,
        qpiece,
        opiece,
        jnp.asarray(order),
        jnp.asarray(pick),
        jnp.asarray(rowtab),
        jnp.asarray(coltab),
    )
    return tuple(o.reshape(2, 1, 2048) for o in outs)


def solution(mesh):
    return jax.shard_map(
        body,
        mesh=mesh,
        in_specs=(
            P("item", "rows", None),
            P("item"),
            P("item"),
            P("item"),
            P(),
            P(),
            P("item", None, None, "hid"),
            P(),
            P(None, ("item", "rows"), "hid"),
            P("hid", ("item", "rows")),
            P(),
        ),
        out_specs=(P("item", "rows", None), P("item", "rows", None)),
        check_vma=False,
    )
```

time: 423 us -> 65.5 us (0.15)
  waiting for transfers between devices: 367 us -> 0 us
  Pallas kernels: 0 us -> 55.1 us
  matrix products: 14.3 us -> 0 us
  local copies, waits for them, and re-layouts: 21.5 us -> 7.34 us
  between operations: 14.8 us -> 1.38 us
  other arithmetic: 5.08 us -> 0.61 us
    all_gather x3 -> x0, waiting for transfers between devices: 332 us -> none  [the longest x1 137 us: body(): lax.all_gather(qkv_weight, ('item', 'rows'), axis=1, tiled=True)]
    pallas_call x0 -> x1, Pallas kernels: none -> 55.1 us  [body(): pl.pallas_call(kernel, out_shape=(shape, shape), in_specs=[smem] * 4 + [v...]
    psum x1 -> x0, waiting for transfers between devices: 34.3 us -> none  [body(): lax.psum(partial_value.astype(jnp.bfloat16), 'hid').astype(jnp.float32)]
    dot_general x9 -> x0, matrix products: 14.3 us -> none  [the longest x1 3.42 us: body(): jnp.einsum('sqhd,skhd->shqk', queries, key_piece, preferred_element_type=...]
    another operation x3 -> x0, local copies, waits for them, and re-layouts: 9.75 us -> none  [the longest x1 5.89 us: body(): gathered[1].reshape(slot_count, key_rows * col_count, heads_here, HD)]
    slice x6 -> x4, local copies, waits for them, and re-layouts: 5.78 us -> 0.72 us  [body(): w = jnp.stack([qkv_weight[1], qkv_weight[2], qkv_weight[0]])]
  transfers between devices with their start and end apart: 4 -> 0, of which waited for: 4 -> 0; matrix products, arithmetic and copies ran while one was open for 3% -> 0% of each run, Pallas kernels for 0% -> 0%
where the time goes in v1:
time: 65.5 us; the launch traced here: 64.5 us
  Pallas kernels  55.1 us (84%)
  local copies, waits for them, and re-layouts  7.34 us (11%)
  between operations  1.38 us (2%)
    pallas_call x1, Pallas kernels, body(): pl.pallas_call(kernel, out_shape=(shape, shape), in_specs=[smem] * 4 + [v...  55.1 us
    unnamed x13, local copies, waits for them, and re-layouts  5.16 us

profile of v1, /device:TPU:1, one launch (start us, length us, event | category | flops | bytes accessed | tf_op | source)
XLA Modules:
  0.0 64.5 jit_solution(1741744620016142272)
XLA Ops:
  0.6 0.0 copy-start.3
  1.3 0.0 copy-done.3
  1.3 0.0 copy-start.1
  1.3 0.6 pad.14.opiece
  1.9 0.1 copy-done.1
  2.1 0.6 convert_element_type.9.latb
  2.7 0.0 slice-start
  2.7 0.0 slice-start.1
  2.7 0.7 %slice-done = bf16[1,6,384]{2,1,0:T(8,128)(2,1)S(1)} async-done(((bf16[3,6,384]{2,1,0:T(8,128)(2,1)}), bf16[1,6,384]{2,1,0:T(8,128)(2,1)S(1)}, s32[]{:S(2)}) %slice-start) | async-done | bytes 4632 | tf_op jit(solution)/shard_map/slice | solution.py:495
  3.3 0.0 slice-done.1
  3.4 0.1 reshape.32
  3.5 0.1 reshape.33
  3.7 0.0 copy-start
  3.7 0.6 pad.13.qpiece
  4.3 1.9 %copy.36.text = bf16[2,2,154,384]{3,2,1,0:T(8,128)(2,1)} copy(bf16[2,2,154,384]{3,1,2,0:T(2,128)(2,1)} %param.21) | data formatting | bytes 946176 | tf_op args[6]
  6.2 0.0 copy-done
  6.2 1.2 %copy.35.cond = f32[16,5,1536]{2,1,0:T(8,128)} copy(f32[16,5,1536]{2,0,1:T(8,128)S(1)} %copy-done) | data formatting | bytes 983040 | tf_op args[5]
  7.4 55.1 %shard_map.158 = (f32[2,16,128]{2,1,0:T(8,128)}, f32[2,16,128]{2,1,0:T(8,128)}) custom-call(s32[2]{0:T(128)} %heights.1, s32[2]{0:T(128)} %widths.1, s32[2]{0:T(128)} %slot_item.1, s32[1]{0:T(128)S(6)} %copy.44.step_index, f32[2,16,128]{2,1,0:T(8,128)} %bitcast.21, bf16[2,16,128]{2,1,0:T(8,128)(2,1)} %convert_element_type.9.latb, f32[16,5,1536]{2,1,0:T(8,128)} %copy.35.cond, ...), custom_call_target="tpu_custom_call" | custom-call | tf_op jit(solution)/shard_map/pallas_call | solution.py:505
  62.5 0.0 copy-start.2
  62.5 1.3 %copy.45 = f32[2,1,2048]{2,1,0:T(1,128)} copy(f32[2,1,2048]{2,1,0:T(1,128)} %bitcast.25) | data formatting | bytes 32768
  63.8 0.0 copy-done.2
  63.9 0.6 copy.46
  (7 shorter events, 0.1 us)
Async XLA Ops:
  0.6 0.7 %copy-start.3 = (bf16[384,6]{0,1:T(8,128)(2,1)S(1)}, bf16[384,6]{0,1:T(8,128)(2,1)}, u32[]{:S(2)}) copy-start(bf16[384,6]{0,1:T(8,128)(2,1)} %param.24) | copy-start | bytes 13828
  1.3 0.7 %copy-start.1 = (f32[2,1,2048]{2,1,0:T(1,128)S(1)}, f32[2,1,2048]{2,1,0:T(1,128)}, u32[]{:S(2)}) copy-start(f32[2,1,2048]{2,1,0:T(1,128)} %param.15) | copy-start | bytes 49156
  2.7 0.7 %slice-start = ((bf16[3,6,384]{2,1,0:T(8,128)(2,1)}), bf16[1,6,384]{2,1,0:T(8,128)(2,1)S(1)}, s32[]{:S(2)}) async-start(bf16[3,6,384]{2,1,0:T(8,128)(2,1)} %param.23), calls=%async_computation | async-start | bytes 12288 | tf_op jit(solution)/shard_map/slice | solution.py:495
  2.7 0.7 %slice-start.1 = ((bf16[3,6,384]{2,1,0:T(8,128)(2,1)}), bf16[2,6,384]{2,1,0:T(8,128)(2,1)S(1)}, s32[]{:S(2)}) async-start(bf16[3,6,384]{2,1,0:T(8,128)(2,1)} %param.23), calls=%async_computation.1 | async-start | bytes 24576 | tf_op jit(solution)/shard_map/slice | solution.py:495
  3.7 2.5 %copy-start = (f32[16,5,1536]{2,0,1:T(8,128)S(1)}, f32[16,5,1536]{2,0,1:T(8,128)}, u32[]{:S(2)}) copy-start(f32[16,5,1536]{2,0,1:T(8,128)} %param.20) | copy-start | bytes 1474564
  62.5 1.3 %copy-start.2 = (f32[2,16,128]{2,1,0:T(8,128)S(1)}, f32[2,16,128]{2,1,0:T(8,128)}, u32[]{:S(2)}) copy-start(f32[2,16,128]{2,1,0:T(8,128)} %get-tuple-element.5) | copy-start | bytes 49156

commit v2 on v1

--- a/solution.py
+++ b/solution.py
@@ -51,6 +51,11 @@
     return order[None, :], pick, row_table[:, None, :], col_table
 
 
+def sigma_level(position):
+    fraction = 1.0 - position / STEPS
+    return 3.0 * fraction / (1.0 + 2.0 * fraction)
+
+
 def relative_partners():
     found = set()
     for dy in range(NY):
@@ -70,21 +75,33 @@
     heights,
     widths,
     slot_item,
-    step_index,
+    lat_in,
+    cond_in,
+    text_in,
+    wp_in,
+    wft_in,
+    wq_in,
+    wo_in,
+    order_in,
+    pick_in,
+    rowtab_in,
+    coltab_in,
+    vel_out,
     lat,
-    latb,
     cond,
     text,
     wp,
     wft,
-    qpiece,
-    opiece,
+    wq,
+    wo,
     order,
     pick,
     rowtab,
     coltab,
-    next_out,
-    den_out,
+    latb,
+    qpiece,
+    opiece,
+    piece,
     lb,
     qb,
     ob,
@@ -100,6 +117,7 @@
     eb,
     send_att,
     recv_att,
+    sem_in,
     sem_ls,
     sem_lr,
     sem_qs,
@@ -147,6 +165,38 @@
             device_id=device((y + dy) % 8, (z + dz) % 8, flip(xh, dxh), flip(core, dc), flip(xl, dxl)),
             device_id_type=MESH,
         )
+    pairs = (
+        (wq_in, wq),
+        (wo_in, wo),
+        (lat_in, lat),
+        (wp_in, wp),
+        (wft_in, wft),
+        (order_in, order),
+        (pick_in, pick),
+        (cond_in, cond),
+        (rowtab_in, rowtab),
+        (coltab_in, coltab),
+        (text_in.at[core], text),
+    )
+    loads = [pltpu.make_async_copy(a, b, sem_in.at[i]) for i, (a, b) in enumerate(pairs)]
+    for load in loads:
+        load.start()
+    loads[0].wait()
+    for q in range(2):
+        cut = slice(q * 192, (q + 1) * 192)
+        parts = [wq[i].astype(F32)[:, cut] for i in (1, 2, 0)]
+        full = jnp.concatenate(parts + [jnp.zeros((6, 64), F32)], 1)
+        for t in range(5):
+            piece[q, t * 6 : t * 6 + 6] = full[:, t * 128 : (t + 1) * 128]
+        piece[q, 30:32] = jnp.zeros((2, 128), F32)
+        qpiece[q] = piece[q].astype(BF16)
+    loads[1].wait()
+    for t in range(3):
+        piece[2, t * 6 : t * 6 + 6] = wo[:, t * 128 : (t + 1) * 128].astype(F32)
+    piece[2, 18:32] = jnp.zeros((14, 128), F32)
+    opiece[...] = piece[2].astype(BF16)
+    loads[2].wait()
+    latb[...] = lat[...].astype(BF16)
     lb[rows] = latb[core]
     qb[by_b * 2 + xh] = qpiece[xh]
     ob[xl * 16 + by_b * 2 + xh] = opiece[...]
@@ -192,29 +242,13 @@
                     )
                 )
                 l_copies[-1].start()
-    for k in range(8):
-        for dxh in range(2):
-            for dxl in range(2):
-                n = k * 4 + dxh * 2 + dxl
-                if n == 0:
-                    continue
-                ty, tz = ring_b(k)
-                o_copies.append(
-                    remote(
-                        opiece,
-                        ob.at[xl * 16 + by_b * 2 + xh],
-                        sem_os.at[n],
-                        sem_or.at[n],
-                        device(ty, tz, flip(xh, dxh), core, flip(xl, dxl)),
-                    )
-                )
-                o_copies[-1].start()
-
+    for load in loads[3:]:
+        load.wait()
     eb[...] = (lax.broadcasted_iota(jnp.int32, (480, 512), 1) == pick[...]).astype(F32).astype(BF16)
     rows_in[0:64] = wp[...]
     rows_in[64:128] = wft[...]
     for s in range(2):
-        c = cond[slot_item[s]]
+        c = jnp.concatenate([cond[i, pl.ds(slot_item[s], 1)] for i in range(5)], 0)
         hi = c.astype(BF16)
         mid = (c - hi.astype(F32)).astype(BF16)
         low = (c - hi.astype(F32) - mid.astype(F32)).astype(BF16)
@@ -260,12 +294,12 @@
             self.sent, self.come = [], {}
             self.partner = []
 
-        def send(self, n, origin, step):
+        def send(self, n, origin, step, part=slice(None)):
             ty, tz = ring_c((step + 8) % 8)
-            slot = unit(origin)
+            block = self.buf.at[unit(origin), part]
             c = remote(
-                self.buf.at[slot],
-                self.buf.at[slot],
+                block,
+                block,
                 self.s.at[n],
                 self.r.at[n],
                 device(ty, tz, xh, core, xl),
@@ -296,9 +330,10 @@
         def second(self):
             self.come[0].wait_recv()
             self.send(4, -2, 1)
-            self.send(6, -2, 2)
+            self.send(6, -2, 2, slice(0, 48))
             self.come[1].wait_recv()
             self.send(5, 2, -1)
+            self.send(7, 2, -2, slice(48, 96))
             self.share(1, -2)
             self.share(2, 2)
             self.come[2].wait_recv()
@@ -312,6 +347,7 @@
             self.come[5].wait_recv()
             self.share(6, 3)
             self.come[6].wait_recv()
+            self.come[7].wait_recv()
             self.share(7, -4)
 
         def last(self):
@@ -324,6 +360,34 @@
 
     qs = Spread(qu, sem_us, sem_ur, sem_ps, sem_pr)
     qs.first()
+    for k in range(8):
+        for dxh in range(2):
+            for dxl in range(2):
+                n = k * 4 + dxh * 2 + dxl
+                if n == 0:
+                    continue
+                ty, tz = ring_b(k)
+                o_copies.append(
+                    remote(
+                        opiece,
+                        ob.at[xl * 16 + by_b * 2 + xh],
+                        sem_os.at[n],
+                        sem_or.at[n],
+                        device(ty, tz, flip(xh, dxh), core, flip(xl, dxl)),
+                    )
+                )
+                o_copies[-1].start()
+
+
+    r_id = lax.broadcasted_iota(jnp.int32, (384, 384), 0)
+    c_id = lax.broadcasted_iota(jnp.int32, (384, 384), 1)
+    pick_key = ((r_id == c_id + 192 * xh) & (c_id < 192)).astype(F32).astype(BF16)
+    pick_val = ((r_id == c_id - 192 + 192 * xh) & (c_id >= 192)).astype(F32).astype(BF16)
+    place = ((r_id - 192 + 192 * xh == c_id) & (r_id >= 192)).astype(F32).astype(BF16)
+    text_rows = (
+        jnp.dot(text[:, 0], pick_key, preferred_element_type=F32)
+        + jnp.dot(text[:, 1], pick_val, preferred_element_type=F32)
+    ).astype(BF16)
 
     def normalise(value):
         mean = jnp.mean(value, -1, keepdims=True)
@@ -376,16 +440,6 @@
     ).astype(BF16)
     queries = jnp.concatenate([queries, jnp.zeros((128, 128), BF16)], 1)
     ws.second()
-
-    r_id = lax.broadcasted_iota(jnp.int32, (384, 384), 0)
-    c_id = lax.broadcasted_iota(jnp.int32, (384, 384), 1)
-    pick_key = ((r_id == c_id + 192 * xh) & (c_id < 192)).astype(F32).astype(BF16)
-    pick_val = ((r_id == c_id - 192 + 192 * xh) & (c_id >= 192)).astype(F32).astype(BF16)
-    place = ((r_id - 192 + 192 * xh == c_id) & (r_id >= 192)).astype(F32).astype(BF16)
-    text_rows = (
-        jnp.dot(text[core, 0], pick_key, preferred_element_type=F32)
-        + jnp.dot(text[core, 1], pick_val, preferred_element_type=F32)
-    ).astype(BF16)
 
     height, width = heights[core], widths[core]
     key_id = lax.broadcasted_iota(jnp.int32, (1, 1024), 1)
@@ -436,15 +490,6 @@
     for copy in a_copies:
         copy.wait_recv()
 
-    step = jnp.zeros((1, 128), F32) + step_index[0].astype(F32)
-
-    def sigma_level(position):
-        fraction = 1.0 - position / STEPS
-        return 3.0 * fraction / (1.0 + 2.0 * fraction)
-
-    sigma_now = sigma_level(step)
-    sigma_next = sigma_level(step + 1.0)
-
     halves = [
         jnp.concatenate([recv_att[s, 2 * g] + recv_att[s, 2 * g + 1] for s in range(2)], 0) for g in range(2)
     ]
@@ -466,9 +511,7 @@
         l_id = lax.broadcasted_iota(jnp.int32, (16, 128), 1)
         row_live = jnp.where(rows < heights[s], 1, 0)
         alive = (m_id * 2 + l_id // 64 < widths[s] * row_live)
-        velocity = jnp.where(alive, velocity, 0.0)
-        next_out[s] = lat[s] + (sigma_next - sigma_now) * velocity
-        den_out[s] = lat[s] - sigma_now * velocity
+        vel_out[s] = jnp.where(alive, velocity, 0.0)
 
     for copy in q_copies + l_copies + o_copies + a_copies:
         copy.wait_send()
@@ -490,24 +533,31 @@
     final_weight,
 ):
     order, pick, rowtab, coltab = tables()
-    lat = latents.reshape(2, 16, 128)
-    latb = lat.astype(BF16)
-    w = jnp.stack([qkv_weight[1], qkv_weight[2], qkv_weight[0]])
-    w = w.reshape(3, 6, 2, 192).transpose(2, 1, 0, 3).reshape(2, 6, 576)
-    w = jnp.pad(w, ((0, 0), (0, 0), (0, 64))).reshape(2, 6, 5, 128).transpose(0, 2, 1, 3)
-    qpiece = jnp.pad(w.reshape(2, 30, 128), ((0, 0), (0, 2), (0, 0)))
-    o = out_weight.T.reshape(6, 3, 128).transpose(1, 0, 2).reshape(18, 128)
-    opiece = jnp.pad(o, ((0, 14), (0, 0)))
     smem = pl.BlockSpec(memory_space=pltpu.SMEM)
     vmem = pl.BlockSpec(memory_space=pltpu.VMEM)
     dma = pltpu.SemaphoreType.DMA
     shape = jax.ShapeDtypeStruct((2, 16, 128), F32)
-    outs = pl.pallas_call(
+    velocity = pl.pallas_call(
         kernel,
-        out_shape=(shape, shape),
-        in_specs=[smem] * 4 + [vmem] * 12,
-        out_specs=(vmem, vmem),
+        out_shape=shape,
+        in_specs=[smem] * 3 + [pl.BlockSpec(memory_space=pl.ANY)] * 11,
+        out_specs=vmem,
         scratch_shapes=[
+            pltpu.VMEM((2, 16, 128), F32),
+            pltpu.VMEM((5, 16, D), F32),
+            pltpu.VMEM((154, 2, 384), BF16),
+            pltpu.VMEM((64, D), BF16),
+            pltpu.VMEM((64, D), BF16),
+            pltpu.VMEM((3, 6, 384), BF16),
+            pltpu.VMEM((6, 384), BF16),
+            pltpu.VMEM(order.shape, jnp.int32),
+            pltpu.VMEM(pick.shape, jnp.int32),
+            pltpu.VMEM(rowtab.shape, F32),
+            pltpu.VMEM(coltab.shape, F32),
+            pltpu.VMEM((2, 16, 128), BF16),
+            pltpu.VMEM((2, 32, 128), BF16),
+            pltpu.VMEM((32, 128), BF16),
+            pltpu.VMEM((3, 32, 128), F32),
             pltpu.VMEM((32, 16, 128), BF16),
             pltpu.VMEM((16, 32, 128), BF16),
             pltpu.VMEM((32, 32, 128), BF16),
@@ -524,7 +574,7 @@
             pltpu.VMEM((4, 32, 384), BF16),
             pltpu.VMEM((2, 4, 32, 384), BF16),
         ]
-        + [dma((n,)) for n in (32, 32, 16, 16, 32, 32, 7, 7, 8, 8, 7, 7, 8, 8, 8, 8)],
+        + [dma((n,)) for n in (11, 32, 32, 16, 16, 32, 32, 8, 8, 8, 8, 8, 8, 8, 8, 8, 8)],
         compiler_params=pltpu.CompilerParams(
             collective_id=0, has_side_effects=True, vmem_limit_bytes=56 * 1024 * 1024
         ),
@@ -532,21 +582,22 @@
         heights,
         widths,
         slot_item,
-        step_index,
-        lat,
-        latb,
-        cond_table,
-        text_kv,
+        latents.reshape(2, 16, 128),
+        cond_table.transpose(1, 0, 2),
+        text_kv.transpose(0, 2, 1, 3),
         patch_weight,
         final_weight.T,
-        qpiece,
-        opiece,
+        qkv_weight,
+        out_weight.T,
         jnp.asarray(order),
         jnp.asarray(pick),
         jnp.asarray(rowtab),
         jnp.asarray(coltab),
-    )
-    return tuple(o.reshape(2, 1, 2048) for o in outs)
+    ).reshape(2, 1, 2048)
+    position = step_index[0].astype(F32)
+    sigma_now = sigma_level(position)
+    sigma_next = sigma_level(position + 1.0)
+    return latents + (sigma_next - sigma_now) * velocity, latents - sigma_now * velocity
 
 
 def solution(mesh):

time: 65.5 us -> 58.7 us (0.90); the launches traced: 64.5 us -> 58.5 us
  local copies, waits for them, and re-layouts: 7.34 us -> 0.01 us
  other arithmetic: 0.61 us -> 1.37 us
    unnamed x13 -> x2, local copies, waits for them, and re-layouts: 5.16 us -> 0.01 us
    pad x2 -> x0, local copies, waits for them, and re-layouts: 1.21 us -> none  [the longest x1 0.61 us: body(): qpiece = jnp.pad(w.reshape(2, 30, 128), ((0, 0), (0, 2), (0, 0)))]
    mul x0 -> x1, other arithmetic: none -> 0.73 us  [body(): sigma_now * velocity]
    slice x4 -> x0, local copies, waits for them, and re-layouts: 0.72 us -> none  [body(): w = jnp.stack([qkv_weight[1], qkv_weight[2], qkv_weight[0]])]
where the time goes in v2:
time: 58.7 us; the launch traced here: 58.5 us
  Pallas kernels  55.7 us (95%)
  between operations  1.39 us (2%)
  other arithmetic  1.37 us (2%)
    pallas_call x1, Pallas kernels, body(): pl.pallas_call(kernel, out_shape=shape, in_specs=[smem] * 3 + [pl.BlockSp...  55.7 us

profile of v2, /device:TPU:1, one launch (start us, length us, event | category | flops | bytes accessed | tf_op | source)
XLA Modules:
  0.0 58.5 jit_solution(13750223263393310732)
XLA Ops:
  1.4 55.7 %shard_map.158 = f32[2,16,128]{2,1,0:T(8,128)} custom-call(s32[2]{0:T(128)} %heights.1, s32[2]{0:T(128)} %widths.1, s32[2]{0:T(128)} %slot_item.1, f32[2,16,128]{2,1,0:T(8,128)} %bitcast.12, f32[5,16,1536]{2,1,0:T(8,128)} %bitcast.9, bf16[2,154,2,384]{3,2,1,0:T(2,128)(2,1)} %bitcast.10, bf16[64,1536]{1,0:T(8,128)(2,1)} %wp_in.1, bf16[64,1536]{1,0:T(8,128)(2,1)} %bitcast.11, ...), custom_call_target="tpu_custom_call" | custom-call | tf_op jit(solution)/shard_map/pallas_call | solution.py:540
  57.1 0.0 copy-start
  57.1 0.7 %broadcast_multiply_fusion = (f32[2,16,128]{2,1,0:T(8,128)S(1)}, f32[2,16,128]{2,1,0:T(8,128)S(1)}) fusion(f32[2,16,128]{2,1,0:T(8,128)} %shard_map.158, f32[]{:T(128)} %bitcast.1, f32[]{:T(128)S(6)} %sub.19), kind=kLoop, calls=%fused_computation | loop fusion | flops 8192 | bytes 49160 | tf_op jit(solution)/shard_map/mul | solution.py:600
  57.9 0.0 copy-done
  57.9 0.6 %fusion = (f32[2,1,2048]{2,1,0:T(1,128)}, f32[2,1,2048]{2,1,0:T(1,128)}) fusion(f32[2,1,2048]{2,1,0:T(1,128)S(1)} %copy-done, f32[2,1,2048]{2,1,0:T(1,128)S(1)} %bitcast.13, f32[2,1,2048]{2,1,0:T(1,128)S(1)} %bitcast.14), kind=kLoop, calls=%fused_computation.2 | loop fusion | flops 8192 | bytes 81920 | tf_op jit(solution)/shard_map/sub | solution.py:600
Async XLA Ops:
  57.1 0.7 %copy-start = (f32[2,1,2048]{2,1,0:T(1,128)S(1)}, f32[2,1,2048]{2,1,0:T(1,128)}, u32[]{:S(2)}) copy-start(f32[2,1,2048]{2,1,0:T(1,128)} %param.15) | copy-start | bytes 49156

commit v3 on v2

--- a/solution.py
+++ b/solution.py
@@ -47,8 +47,24 @@
         for source in range(16):
             for j in range(6):
                 pick[tile * 96 + source * 6 + j, 0] = source * 32 + tile * 6 + j
+    pick_out = np.zeros((144, 1), np.int32)
+    for tile in range(3):
+        for source in range(16):
+            for j in range(3):
+                pick_out[tile * 48 + source * 3 + j, 0] = source * 16 + tile * 3 + j
     col_table = np.stack([col_table[0::2], col_table[1::2]])
-    return order[None, :], pick, row_table[:, None, :], col_table
+    place = np.arange(D).reshape(256, 2, 3)
+    halves = np.stack([place[:, h].reshape(-1) for h in range(2)])
+    return (
+        order[None, :],
+        pick,
+        row_table[:, None, :],
+        col_table,
+        order[halves][:, None, :],
+        pick_out,
+        np.stack([row_table[:, None, half] for half in halves]),
+        np.stack([col_table[:, :, half] for half in halves]),
+    )
 
 
 def sigma_level(position):
@@ -63,7 +79,7 @@
             for dxh in range(2):
                 for dc in range(2):
                     for dxl in range(2):
-                        near = (dy == 0 and dxl == 0) or (dy == 0 and dz == 0)
+                        near = (dy == 0 and dxl == 0 and dxh == 0) or (dy == 0 and dz == 0)
                         near = near or (dc == 0 and (dy == 0 or dz == 0))
                         if near:
                             found.add((dy, dz, dxh, dc, dxl))
@@ -72,9 +88,9 @@
 
 
 def kernel(
-    heights,
-    widths,
-    slot_item,
+    heights_in,
+    widths_in,
+    slot_in,
     lat_in,
     cond_in,
     text_in,
@@ -86,7 +102,14 @@
     pick_in,
     rowtab_in,
     coltab_in,
+    order_h_in,
+    pick_o_in,
+    rowtab_h_in,
+    coltab_h_in,
     vel_out,
+    heights,
+    widths,
+    slot_item,
     lat,
     cond,
     text,
@@ -98,6 +121,10 @@
     pick,
     rowtab,
     coltab,
+    order_h,
+    pick_o,
+    rowtab_h,
+    coltab_h,
     latb,
     qpiece,
     opiece,
@@ -110,13 +137,21 @@
     nb,
     kvb,
     wps,
-    wfs,
+    wph,
+    wfh,
     cperm,
+    chalf,
+    split,
+    sums_in,
     rows_in,
     rows_out,
+    rows_half,
     eb,
+    eo,
     send_att,
     recv_att,
+    pay,
+    got_pay,
     sem_in,
     sem_ls,
     sem_lr,
@@ -134,6 +169,10 @@
     sem_xr,
     sem_as,
     sem_ar,
+    sem_bs,
+    sem_br,
+    sem_fs,
+    sem_fr,
 ):
     y = lax.axis_index("item")
     rows = lax.axis_index("rows")
@@ -177,6 +216,13 @@
         (rowtab_in, rowtab),
         (coltab_in, coltab),
         (text_in.at[core], text),
+        (order_h_in.at[xl], order_h),
+        (pick_o_in, pick_o),
+        (rowtab_h_in.at[xl], rowtab_h),
+        (coltab_h_in.at[xl], coltab_h),
+        (heights_in, heights),
+        (widths_in, widths),
+        (slot_in, slot_item),
     )
     loads = [pltpu.make_async_copy(a, b, sem_in.at[i]) for i, (a, b) in enumerate(pairs)]
     for load in loads:
@@ -191,15 +237,18 @@
         piece[q, 30:32] = jnp.zeros((2, 128), F32)
         qpiece[q] = piece[q].astype(BF16)
     loads[1].wait()
-    for t in range(3):
-        piece[2, t * 6 : t * 6 + 6] = wo[:, t * 128 : (t + 1) * 128].astype(F32)
-    piece[2, 18:32] = jnp.zeros((14, 128), F32)
-    opiece[...] = piece[2].astype(BF16)
+    for half in range(2):
+        for t in range(3):
+            at = half * 16 + t * 3
+            piece[2, at : at + 3] = wo[...].astype(F32)[half * 3 : half * 3 + 3, t * 128 : (t + 1) * 128]
+        piece[2, half * 16 + 9 : half * 16 + 16] = jnp.zeros((7, 128), F32)
+        opiece[half] = piece[2, half * 16 : half * 16 + 16].astype(BF16)
     loads[2].wait()
     latb[...] = lat[...].astype(BF16)
-    lb[rows] = latb[core]
+    my_lat = xh * 16 + z * 2 + core
+    lb[my_lat] = latb[core]
     qb[by_b * 2 + xh] = qpiece[xh]
-    ob[xl * 16 + by_b * 2 + xh] = opiece[...]
+    ob[xl * 16 + by_b * 2 + xh] = opiece[xl]
     pl.semaphore_wait(barrier, len(partners))
 
     def remote(src, dst, s_sem, r_sem, to):
@@ -226,57 +275,25 @@
             )
             q_copies[-1].start()
     for dz in range(8):
-        for dxh in range(2):
-            for dc in range(2):
-                n = dz * 4 + dxh * 2 + dc
-                if n == 0:
-                    continue
-                tc = flip(core, dc)
-                l_copies.append(
-                    remote(
-                        latb.at[tc],
-                        lb.at[rows],
-                        sem_ls.at[n],
-                        sem_lr.at[n],
-                        device(y, (z + dz) % 8, flip(xh, dxh), tc, xl),
-                    )
+        for dc in range(2):
+            n = dz * 2 + dc
+            if n == 0:
+                continue
+            tc = flip(core, dc)
+            l_copies.append(
+                remote(
+                    latb.at[tc],
+                    lb.at[my_lat],
+                    sem_ls.at[n],
+                    sem_lr.at[n],
+                    device(y, (z + dz) % 8, xh, tc, xl),
                 )
-                l_copies[-1].start()
+            )
+            l_copies[-1].start()
     for load in loads[3:]:
         load.wait()
     eb[...] = (lax.broadcasted_iota(jnp.int32, (480, 512), 1) == pick[...]).astype(F32).astype(BF16)
-    rows_in[0:64] = wp[...]
-    rows_in[64:128] = wft[...]
-    for s in range(2):
-        c = jnp.concatenate([cond[i, pl.ds(slot_item[s], 1)] for i in range(5)], 0)
-        hi = c.astype(BF16)
-        mid = (c - hi.astype(F32)).astype(BF16)
-        low = (c - hi.astype(F32) - mid.astype(F32)).astype(BF16)
-        zero = jnp.zeros((3, D), F32)
-        for i, piece in enumerate((hi, mid, low)):
-            at = 128 + s * 24 + i * 8
-            cperm[at - 128 : at - 120] = jnp.concatenate([piece.astype(F32), zero], 0)
-    rows_in[128:176] = cperm[0:48].astype(BF16)
-    for i in range(6):
-        cols = slice(i * 256, (i + 1) * 256)
-        onehot = (
-            (lax.broadcasted_iota(jnp.int32, (D, 256), 0) == order[:, cols]).astype(F32).astype(BF16)
-        )
-        rows_out[:, cols] = jnp.dot(rows_in[...], onehot, preferred_element_type=F32)
-    blank = jnp.zeros((64, D), BF16)
-    wps[0, 0:64] = rows_out[0:64].astype(BF16)
-    wps[0, 64:128] = blank
-    wps[1, 0:64] = blank
-    wps[1, 64:128] = rows_out[0:64].astype(BF16)
-    wfs[0, 0:64] = rows_out[64:128].astype(BF16)
-    wfs[0, 64:128] = blank
-    wfs[1, 0:64] = blank
-    wfs[1, 64:128] = rows_out[64:128].astype(BF16)
-    for s in range(2):
-        at = 128 + s * 24
-        cperm[s * 8 : s * 8 + 8] = (
-            rows_out[at : at + 8] + rows_out[at + 8 : at + 16] + rows_out[at + 16 : at + 24]
-        )
+    eo[...] = (lax.broadcasted_iota(jnp.int32, (144, 256), 1) == pick_o[...]).astype(F32).astype(BF16)
 
     for copy in q_copies:
         copy.wait_recv()
@@ -291,6 +308,7 @@
     class Spread:
         def __init__(self, buf, s_sem, r_sem, ps_sem, pr_sem):
             self.buf, self.s, self.r, self.ps, self.pr = buf, s_sem, r_sem, ps_sem, pr_sem
+            self.cut = buf.shape[1] // 32 * 16 + buf.shape[1] % 32
             self.sent, self.come = [], {}
             self.partner = []
 
@@ -330,10 +348,10 @@
         def second(self):
             self.come[0].wait_recv()
             self.send(4, -2, 1)
-            self.send(6, -2, 2, slice(0, 48))
+            self.send(6, -2, 2, slice(0, self.cut))
             self.come[1].wait_recv()
             self.send(5, 2, -1)
-            self.send(7, 2, -2, slice(48, 96))
+            self.send(7, 2, -2, slice(self.cut, None))
             self.share(1, -2)
             self.share(2, 2)
             self.come[2].wait_recv()
@@ -369,7 +387,7 @@
                 ty, tz = ring_b(k)
                 o_copies.append(
                     remote(
-                        opiece,
+                        opiece.at[flip(xl, dxl)],
                         ob.at[xl * 16 + by_b * 2 + xh],
                         sem_os.at[n],
                         sem_or.at[n],
@@ -379,11 +397,62 @@
                 o_copies[-1].start()
 
 
+    for copy in l_copies:
+        copy.wait_recv()
+    block = lb.at[pl.ds(pl.multiple_of(xh * 16, 16), 16)]
+    b_copy = remote(block, block, sem_bs.at[0], sem_br.at[0], device(y, z, 1 - xh, core, xl))
+    b_copy.start()
+
+    rows_in[0:64] = wp[...]
+    rows_in[112:176] = wft[...]
+
+    def three(value):
+        hi = value.astype(BF16).astype(F32)
+        mid = (value - hi).astype(BF16).astype(F32)
+        return hi, mid, (value - hi - mid).astype(BF16).astype(F32)
+
+    in_first = (lax.broadcasted_iota(jnp.int32, (1, D), 1) % 6) < 3
+    for s in range(2):
+        c = jnp.concatenate([cond[i, pl.ds(slot_item[s], 1)] for i in range(5)], 0)
+        for i, part in enumerate(three(c)):
+            at = s * 24 + i * 8
+            split[at : at + 8] = jnp.concatenate([part, jnp.zeros((3, D), F32)], 0)
+        scale_f = 1.0 + c[4:5]
+        first = jnp.where(in_first, scale_f, 0.0)
+        three_rows = jnp.concatenate([first, scale_f - first, c[3:4]], 0)
+        parts = three(three_rows)
+        sums_in[s * 16 : s * 16 + 16] = jnp.concatenate(list(parts) + [jnp.zeros((7, D), F32)], 0)
+    rows_in[64:112] = split[...].astype(BF16)
+
+    def onehot(names):
+        return (lax.broadcasted_iota(jnp.int32, (D, 256), 0) == names).astype(F32).astype(BF16)
+
+    for i in range(6):
+        cols = slice(i * 256, (i + 1) * 256)
+        rows_out[:, cols] = jnp.dot(rows_in[0:112], onehot(order[:, cols]), preferred_element_type=F32)
+    for i in range(3):
+        cols = slice(i * 256, (i + 1) * 256)
+        rows_half[:, cols] = jnp.dot(rows_in[...], onehot(order_h[:, cols]), preferred_element_type=F32)
+    for at, rest in ((0, 64), (1, 0)):
+        wps[at, at * 64 : at * 64 + 64] = rows_out[0:64].astype(BF16)
+        wps[at, rest : rest + 64] = jnp.zeros((64, D), BF16)
+        wph[at, at * 64 : at * 64 + 64] = rows_half[0:64].astype(BF16)
+        wph[at, rest : rest + 64] = jnp.zeros((64, D // 2), BF16)
+        wfh[at, at * 64 : at * 64 + 64] = rows_half[112:176].astype(BF16)
+        wfh[at, rest : rest + 64] = jnp.zeros((64, D // 2), BF16)
+    for s in range(2):
+        at = 64 + s * 24
+        for src, dst in ((rows_out, cperm), (rows_half, chalf)):
+            dst[s * 8 : s * 8 + 8] = src[at : at + 8] + src[at + 8 : at + 16] + src[at + 16 : at + 24]
+    nt = (((1,), (1,)), ((), ()))
+    final_rows = jnp.concatenate([wft[...], wft[...]], 0)
+    sums = lax.dot_general(sums_in[...].astype(BF16), final_rows, nt, preferred_element_type=F32)
+
     r_id = lax.broadcasted_iota(jnp.int32, (384, 384), 0)
     c_id = lax.broadcasted_iota(jnp.int32, (384, 384), 1)
     pick_key = ((r_id == c_id + 192 * xh) & (c_id < 192)).astype(F32).astype(BF16)
     pick_val = ((r_id == c_id - 192 + 192 * xh) & (c_id >= 192)).astype(F32).astype(BF16)
-    place = ((r_id - 192 + 192 * xh == c_id) & (r_id >= 192)).astype(F32).astype(BF16)
+    place = ((r_id - 64 + 192 * xh == c_id) & (r_id >= 64)).astype(F32).astype(BF16)[0:256]
     text_rows = (
         jnp.dot(text[:, 0], pick_key, preferred_element_type=F32)
         + jnp.dot(text[:, 1], pick_val, preferred_element_type=F32)
@@ -394,35 +463,37 @@
         centered = value - mean
         return centered * lax.rsqrt(jnp.mean(centered * centered, -1, keepdims=True) + 1e-06)
 
-    for copy in l_copies:
-        copy.wait_recv()
-
     cmine = cperm[pl.ds(pl.multiple_of(core * 8, 8), 8)]
     shift_a, scale_a = cmine[0:1], 1.0 + cmine[1:2]
 
-    def norm_chunk(i, carry):
-        x = lb[pl.ds(i * 4, 4)].reshape(64, 128)
-        for parity in range(2):
-            e = jnp.dot(x, wps[parity], preferred_element_type=F32)
-            for rr in range(4):
-                part = e[rr * 16 : rr * 16 + 16] + (rowtab[i * 4 + rr] + coltab[parity])
-                at = pl.multiple_of(i * 128 + parity * 64 + rr * 16, 16)
-                nb[pl.ds(at, 16)] = (normalise(part) * scale_a + shift_a).astype(BF16)
-        return carry
-
-    lax.fori_loop(0, 4, norm_chunk, 0)
+    def norm_half(half):
+        def chunk(i, carry):
+            x = lb[pl.ds(half * 16 + i * 4, 4)].reshape(64, 128)
+            for parity in range(2):
+                e = jnp.dot(x, wps[parity], preferred_element_type=F32)
+                for rr in range(4):
+                    row = (i * 2 + rr // 2) * 4 + half * 2 + rr % 2
+                    part = e[rr * 16 : rr * 16 + 16] + (rowtab[row] + coltab[parity])
+                    at = (row // 4) * 128 + parity * 64 + (row % 4) * 16
+                    nb[pl.ds(pl.multiple_of(at, 16), 16)] = (normalise(part) * scale_a + shift_a).astype(BF16)
+            return carry
+
+        lax.fori_loop(0, 4, chunk, 0)
+
+    norm_half(xh)
     qs.second()
     for copy in o_copies:
         copy.wait_recv()
     for half in range(2):
         got = jnp.dot(
-            eb[0:288], ob[half * 16 : half * 16 + 16].reshape(512, 128), preferred_element_type=F32
+            eo[...], ob[half * 16 : half * 16 + 16].reshape(256, 128), preferred_element_type=F32
         ).astype(BF16)
         for t in range(3):
-            ou[mine, :, half * 384 + t * 128 : half * 384 + (t + 1) * 128] = got[t * 96 : (t + 1) * 96]
-    lax.fori_loop(4, 8, norm_chunk, 0)
+            ou[mine, :, half * 384 + t * 128 : half * 384 + (t + 1) * 128] = got[t * 48 : (t + 1) * 48]
     ws = Spread(ou, sem_ws, sem_wr, sem_xs, sem_xr)
     ws.first()
+    b_copy.wait_recv()
+    norm_half(1 - xh)
     qs.third()
     qs.last()
 
@@ -438,7 +509,6 @@
         qu[:, :, 384:640].reshape(D, 256),
         preferred_element_type=F32,
     ).astype(BF16)
-    queries = jnp.concatenate([queries, jnp.zeros((128, 128), BF16)], 1)
     ws.second()
 
     height, width = heights[core], widths[core]
@@ -446,24 +516,27 @@
     key_row = (key_id // 128) * 4 + (key_id // 16) % 4
     key_col = (key_id % 16) * 2 + (key_id // 64) % 2
     live = (key_row < height) & (key_col < width)
-    lane = lax.broadcasted_iota(jnp.int32, (1, 384), 1)
-    nt = (((1,), (1,)), ((), ()))
-    kv = kvb[...]
-    attended = jnp.zeros((128, 384), F32)
+    lane = lax.broadcasted_iota(jnp.int32, (1, 256), 1)
+    keys, values = kvb[:, 0:256], kvb[:, 128:384]
+    attended = jnp.zeros((128, 256), F32)
+    masked = [
+        jnp.where((lane >= 64 * h) & (lane < 64 * h + 64), queries.astype(F32), 0.0).astype(BF16) for h in range(3)
+    ]
+    stacked = jnp.concatenate(masked, 0)
+    s_text = lax.dot_general(stacked, text_rows[:, 0:256], nt, preferred_element_type=F32) * HD ** (-0.5)
+    s_img = lax.dot_general(stacked, keys, nt, preferred_element_type=F32) * HD ** (-0.5)
+    s_img = jnp.where(live, s_img, -1e30)
+    top = jnp.maximum(jnp.max(s_text, -1, keepdims=True), jnp.max(s_img, -1, keepdims=True))
+    w_text = jnp.exp(s_text - top)
+    w_img = jnp.exp(s_img - top)
+    total = jnp.sum(w_text, -1, keepdims=True) + jnp.sum(w_img, -1, keepdims=True)
+    acc = jnp.dot(w_text.astype(BF16), text_rows[:, 128:384], preferred_element_type=F32) + jnp.dot(
+        w_img.astype(BF16), values, preferred_element_type=F32
+    )
+    acc = acc / total
     for h in range(3):
-        q_h = jnp.where((lane >= 64 * h) & (lane < 64 * h + 64), queries.astype(F32), 0.0).astype(BF16)
-        s_text = lax.dot_general(q_h, text_rows, nt, preferred_element_type=F32) * HD ** (-0.5)
-        s_img = lax.dot_general(q_h, kv, nt, preferred_element_type=F32) * HD ** (-0.5)
-        s_img = jnp.where(live, s_img, -1e30)
-        top = jnp.maximum(jnp.max(s_text, -1, keepdims=True), jnp.max(s_img, -1, keepdims=True))
-        w_text = jnp.exp(s_text - top)
-        w_img = jnp.exp(s_img - top)
-        total = jnp.sum(w_text, -1, keepdims=True) + jnp.sum(w_img, -1, keepdims=True)
-        acc = jnp.dot(w_text.astype(BF16), text_rows, preferred_element_type=F32) + jnp.dot(
-            w_img.astype(BF16), kv, preferred_element_type=F32
-        )
-        inside = (lane >= 192 + 64 * h) & (lane < 256 + 64 * h)
-        attended = attended + jnp.where(inside, acc / total, 0.0)
+        inside = (lane >= 64 + 64 * h) & (lane < 128 + 64 * h)
+        attended = attended + jnp.where(inside, acc[h * 128 : (h + 1) * 128], 0.0)
     placed = jnp.dot(attended.astype(BF16), place, preferred_element_type=F32).astype(BF16)
     for j in range(4):
         for parity in range(2):
@@ -494,26 +567,57 @@
         jnp.concatenate([recv_att[s, 2 * g] + recv_att[s, 2 * g + 1] for s in range(2)], 0) for g in range(2)
     ]
     projected = lax.dot_general(
-        jnp.concatenate(halves, 1), ou[...].reshape(D, 768), nt, preferred_element_type=F32
+        jnp.concatenate(halves, 1), ou[...].reshape(D // 2, 768), nt, preferred_element_type=F32
     )
+    l_id = lax.broadcasted_iota(jnp.int32, (16, 128), 1)
+    stats = jnp.zeros((16, 128), F32)
     for s in range(2):
-        gate = cperm[s * 8 + 2 : s * 8 + 3]
-        shift_f = cperm[s * 8 + 3 : s * 8 + 4]
-        scale_f = 1.0 + cperm[s * 8 + 4 : s * 8 + 5]
-        velocity = jnp.zeros((16, 128), F32)
+        gate = chalf[s * 8 + 2 : s * 8 + 3]
+        scale_f = 1.0 + chalf[s * 8 + 4 : s * 8 + 5]
+        product = jnp.zeros((16, 128), F32)
         for parity in range(2):
-            e = jnp.dot(latb[s], wps[parity], preferred_element_type=F32) + (rowtab[rows] + coltab[parity])
+            e = jnp.dot(latb[s], wph[parity], preferred_element_type=F32) + (rowtab_h[rows] + coltab_h[parity])
             at = s * 32 + parity * 16
             residual = e + gate * projected[at : at + 16]
-            final_in = (normalise(residual) * scale_f + shift_f).astype(BF16)
-            velocity = velocity + lax.dot_general(final_in, wfs[parity], nt, preferred_element_type=F32)
-        m_id = lax.broadcasted_iota(jnp.int32, (16, 128), 0)
-        l_id = lax.broadcasted_iota(jnp.int32, (16, 128), 1)
+            mean = jnp.mean(residual, -1, keepdims=True)
+            centered = residual - mean
+            squares = jnp.sum(centered * centered, -1, keepdims=True)
+            stats = jnp.where(l_id == s * 4 + parity * 2, mean, stats)
+            stats = jnp.where(l_id == s * 4 + parity * 2 + 1, squares, stats)
+            product = product + lax.dot_general(
+                (centered * scale_f).astype(BF16), wfh[parity], nt, preferred_element_type=F32
+            )
+        pay[s] = product
+    pay[2] = stats
+    f_copy = remote(pay, got_pay, sem_fs.at[0], sem_fr.at[0], device(y, z, xh, core, 1 - xl))
+    f_copy.start()
+    f_copy.wait_recv()
+    stats_0 = jnp.where(xl == 0, pay[2], got_pay[2])
+    stats_1 = jnp.where(xl == 0, got_pay[2], pay[2])
+
+    def column(tile, at):
+        even, odd = [jnp.sum(jnp.where(l_id == at + p, tile, 0.0), -1, keepdims=True) for p in (0, 2)]
+        return jnp.where(l_id < 64, even, odd)
+
+    m_id = lax.broadcasted_iota(jnp.int32, (16, 128), 0)
+    for s in range(2):
+        gap = (column(stats_0, s * 4) - column(stats_1, s * 4)) * 0.5
+        squares = column(stats_0, s * 4 + 1) + column(stats_1, s * 4 + 1)
+        slope_0, slope_1, shift = [
+            sums[s * 16 + i : s * 16 + i + 1]
+            + sums[s * 16 + 3 + i : s * 16 + 4 + i]
+            + sums[s * 16 + 6 + i : s * 16 + 7 + i]
+            for i in range(3)
+        ]
+        inverse = lax.rsqrt(squares * (1.0 / D) + gap * gap + 1e-06)
+        velocity = inverse * ((pay[s] + got_pay[s]) + gap * (slope_0 - slope_1)) + shift
         row_live = jnp.where(rows < heights[s], 1, 0)
-        alive = (m_id * 2 + l_id // 64 < widths[s] * row_live)
-        vel_out[s] = jnp.where(alive, velocity, 0.0)
-
-    for copy in q_copies + l_copies + o_copies + a_copies:
+        alive = m_id * 2 + l_id // 64 < widths[s] * row_live
+        velocity = jnp.where(alive, velocity, 0.0)
+        for m in range(16):
+            vel_out[s, :, m * 128 : (m + 1) * 128] = velocity[m : m + 1]
+
+    for copy in q_copies + l_copies + o_copies + a_copies + [b_copy, f_copy]:
         copy.wait_send()
     qs.close()
     ws.close()
@@ -532,17 +636,19 @@
     out_weight,
     final_weight,
 ):
-    order, pick, rowtab, coltab = tables()
-    smem = pl.BlockSpec(memory_space=pltpu.SMEM)
+    constants = tables()
     vmem = pl.BlockSpec(memory_space=pltpu.VMEM)
     dma = pltpu.SemaphoreType.DMA
-    shape = jax.ShapeDtypeStruct((2, 16, 128), F32)
+    shape = jax.ShapeDtypeStruct((2, 1, 2048), F32)
     velocity = pl.pallas_call(
         kernel,
         out_shape=shape,
-        in_specs=[smem] * 3 + [pl.BlockSpec(memory_space=pl.ANY)] * 11,
+        in_specs=[pl.BlockSpec(memory_space=pl.ANY)] * 18,
         out_specs=vmem,
         scratch_shapes=[
+            pltpu.SMEM((2,), jnp.int32),
+            pltpu.SMEM((2,), jnp.int32),
+            pltpu.SMEM((2,), jnp.int32),
             pltpu.VMEM((2, 16, 128), F32),
             pltpu.VMEM((5, 16, D), F32),
             pltpu.VMEM((154, 2, 384), BF16),
@@ -550,31 +656,43 @@
             pltpu.VMEM((64, D), BF16),
             pltpu.VMEM((3, 6, 384), BF16),
             pltpu.VMEM((6, 384), BF16),
-            pltpu.VMEM(order.shape, jnp.int32),
-            pltpu.VMEM(pick.shape, jnp.int32),
-            pltpu.VMEM(rowtab.shape, F32),
-            pltpu.VMEM(coltab.shape, F32),
+            pltpu.VMEM((1, D), jnp.int32),
+            pltpu.VMEM((480, 1), jnp.int32),
+            pltpu.VMEM((32, 1, D), F32),
+            pltpu.VMEM((2, 16, D), F32),
+            pltpu.VMEM((1, D // 2), jnp.int32),
+            pltpu.VMEM((144, 1), jnp.int32),
+            pltpu.VMEM((32, 1, D // 2), F32),
+            pltpu.VMEM((2, 16, D // 2), F32),
             pltpu.VMEM((2, 16, 128), BF16),
             pltpu.VMEM((2, 32, 128), BF16),
-            pltpu.VMEM((32, 128), BF16),
+            pltpu.VMEM((2, 16, 128), BF16),
             pltpu.VMEM((3, 32, 128), F32),
             pltpu.VMEM((32, 16, 128), BF16),
             pltpu.VMEM((16, 32, 128), BF16),
-            pltpu.VMEM((32, 32, 128), BF16),
+            pltpu.VMEM((32, 16, 128), BF16),
             pltpu.VMEM((16, UR, 640), BF16),
-            pltpu.VMEM((16, UR, 768), BF16),
+            pltpu.VMEM((16, UR // 2, 768), BF16),
             pltpu.VMEM((1024, D), BF16),
             pltpu.VMEM((1024, 384), BF16),
             pltpu.VMEM((2, 128, D), BF16),
-            pltpu.VMEM((2, 128, D), BF16),
+            pltpu.VMEM((2, 128, D // 2), BF16),
+            pltpu.VMEM((2, 128, D // 2), BF16),
+            pltpu.VMEM((16, D), F32),
+            pltpu.VMEM((16, D // 2), F32),
             pltpu.VMEM((48, D), F32),
+            pltpu.VMEM((32, D), F32),
             pltpu.VMEM((176, D), BF16),
-            pltpu.VMEM((176, D), F32),
+            pltpu.VMEM((112, D), F32),
+            pltpu.VMEM((176, D // 2), F32),
             pltpu.VMEM((480, 512), BF16),
+            pltpu.VMEM((144, 256), BF16),
             pltpu.VMEM((4, 32, 384), BF16),
             pltpu.VMEM((2, 4, 32, 384), BF16),
+            pltpu.VMEM((3, 16, 128), F32),
+            pltpu.VMEM((3, 16, 128), F32),
         ]
-        + [dma((n,)) for n in (11, 32, 32, 16, 16, 32, 32, 8, 8, 8, 8, 8, 8, 8, 8, 8, 8)],
+        + [dma((n,)) for n in (18, 16, 16, 16, 16, 32, 32, 8, 8, 8, 8, 8, 8, 8, 8, 8, 8, 1, 1, 1, 1)],
         compiler_params=pltpu.CompilerParams(
             collective_id=0, has_side_effects=True, vmem_limit_bytes=56 * 1024 * 1024
         ),
@@ -589,11 +707,8 @@
         final_weight.T,
         qkv_weight,
         out_weight.T,
-        jnp.asarray(order),
-        jnp.asarray(pick),
-        jnp.asarray(rowtab),
-        jnp.asarray(coltab),
-    ).reshape(2, 1, 2048)
+        *[jnp.asarray(constant) for constant in constants],
+    )
     position = step_index[0].astype(F32)
     sigma_now = sigma_level(position)
     sigma_next = sigma_level(position + 1.0)

time: 58.7 us -> 54.1 us (0.922)
  Pallas kernels: 55.7 us -> 50.9 us
    pallas_call x1, Pallas kernels: 55.7 us -> 50.9 us  [body(): pl.pallas_call(kernel, out_shape=shape, in_specs=[pl.BlockSpec(memory_spa...]
    mul x1 -> x0, other arithmetic: 0.73 us -> none  [body(): sigma_now * velocity]
    sub x1, other arithmetic: 0.64 us -> 1.36 us  [body(): latents - sigma_now * velocity]
where the time goes in v3:
time: 54.1 us; the launch traced here: 53.6 us
  Pallas kernels  50.9 us (94%)
  between operations  1.4 us (3%)
  other arithmetic  1.36 us (3%)
    pallas_call x1, Pallas kernels, body(): pl.pallas_call(kernel, out_shape=shape, in_specs=[pl.BlockSpec(memory_spa...  50.9 us
    sub x1, other arithmetic, body(): latents - sigma_now * velocity  1.36 us

profile of v3, /device:TPU:1, one launch (start us, length us, event | category | flops | bytes accessed | tf_op | source)
XLA Modules:
  0.0 53.6 jit_solution(12578835933929647168)
XLA Ops:
  1.4 0.0 copy-start
  1.4 50.9 %shard_map.194 = f32[2,1,2048]{2,1,0:T(1,128)} custom-call(s32[2]{0:T(128)} %heights_in.1, s32[2]{0:T(128)} %widths_in.1, s32[2]{0:T(128)} %slot_in.1, f32[2,16,128]{2,1,0:T(8,128)} %bitcast.10, f32[5,16,1536]{2,1,0:T(8,128)} %bitcast.7, bf16[2,154,2,384]{3,2,1,0:T(2,128)(2,1)} %bitcast.8, bf16[64,1536]{1,0:T(8,128)(2,1)} %wp_in.1, ...), custom_call_target="tpu_custom_call" | custom-call | tf_op jit(solution)/shard_map/pallas_call | solution.py:643
  52.3 0.0 copy-done
  52.3 1.4 %multiply_subtract_fusion = (f32[2,1,2048]{2,1,0:T(1,128)}, f32[2,1,2048]{2,1,0:T(1,128)}) fusion(f32[2,1,2048]{2,1,0:T(1,128)S(1)} %copy-done, f32[2,1,2048]{2,1,0:T(1,128)} %shard_map.194, f32[]{:T(128)} %bitcast.1, f32[]{:T(128)S(6)} %sub.19), kind=kLoop, calls=%fused_computation | loop fusion | flops 16384 | bytes 65544 | tf_op jit(solution)/shard_map/sub | solution.py:715
Async XLA Ops:
  1.4 50.9 %copy-start = (f32[2,1,2048]{2,1,0:T(1,128)S(1)}, f32[2,1,2048]{2,1,0:T(1,128)}, u32[]{:S(2)}) copy-start(f32[2,1,2048]{2,1,0:T(1,128)} %param.19) | copy-start | bytes 49156

commit v4 on v3

--- a/solution.py
+++ b/solution.py
@@ -497,13 +497,7 @@
     qs.third()
     qs.last()
 
-    def kv_chunk(i, carry):
-        at = pl.ds(pl.multiple_of(i * 256, 256), 256)
-        weight = qu[:, :, 0:384].reshape(D, 384)
-        kvb[at] = jnp.dot(nb[at], weight, preferred_element_type=F32).astype(BF16)
-        return carry
-
-    lax.fori_loop(0, 4, kv_chunk, 0)
+    kvb[...] = jnp.dot(nb[...], qu[:, :, 0:384].reshape(D, 384), preferred_element_type=F32).astype(BF16)
     queries = jnp.dot(
         nb[pl.ds(pl.multiple_of(z * 128, 128), 128)],
         qu[:, :, 384:640].reshape(D, 256),
@@ -520,11 +514,11 @@
     keys, values = kvb[:, 0:256], kvb[:, 128:384]
     attended = jnp.zeros((128, 256), F32)
     masked = [
-        jnp.where((lane >= 64 * h) & (lane < 64 * h + 64), queries.astype(F32), 0.0).astype(BF16) for h in range(3)
+        jnp.where((lane >= 64 * h) & (lane < 64 * h + 64), queries.astype(F32) * HD ** (-0.5), 0.0).astype(BF16) for h in range(3)
     ]
     stacked = jnp.concatenate(masked, 0)
-    s_text = lax.dot_general(stacked, text_rows[:, 0:256], nt, preferred_element_type=F32) * HD ** (-0.5)
-    s_img = lax.dot_general(stacked, keys, nt, preferred_element_type=F32) * HD ** (-0.5)
+    s_text = lax.dot_general(stacked, text_rows[:, 0:256], nt, preferred_element_type=F32)
+    s_img = lax.dot_general(stacked, keys, nt, preferred_element_type=F32)
     s_img = jnp.where(live, s_img, -1e30)
     top = jnp.maximum(jnp.max(s_text, -1, keepdims=True), jnp.max(s_img, -1, keepdims=True))
     w_text = jnp.exp(s_text - top)
@@ -533,7 +527,7 @@
     acc = jnp.dot(w_text.astype(BF16), text_rows[:, 128:384], preferred_element_type=F32) + jnp.dot(
         w_img.astype(BF16), values, preferred_element_type=F32
     )
-    acc = acc / total
+    acc = acc * (1.0 / total)
     for h in range(3):
         inside = (lane >= 64 + 64 * h) & (lane < 128 + 64 * h)
         attended = attended + jnp.where(inside, acc[h * 128 : (h + 1) * 128], 0.0)

time: 54.1 us -> 53.4 us (0.987)
  Pallas kernels: 50.9 us -> 50.2 us
    pallas_call x1, Pallas kernels: 50.9 us -> 50.2 us  [body(): pl.pallas_call(kernel, out_shape=shape, in_specs=[pl.BlockSpec(memory_spa...]
where the time goes in v4:
time: 53.4 us; the launch traced here: 53 us
  Pallas kernels  50.2 us (94%)
  between operations  1.4 us (3%)
  other arithmetic  1.36 us (3%)
    pallas_call x1, Pallas kernels, body(): pl.pallas_call(kernel, out_shape=shape, in_specs=[pl.BlockSpec(memory_spa...  50.2 us
    sub x1, other arithmetic, body(): latents - sigma_now * velocity  1.36 us

profile of v4, /device:TPU:1, one launch (start us, length us, event | category | flops | bytes accessed | tf_op | source)
XLA Modules:
  0.0 53.0 jit_solution(14734163852718346229)
XLA Ops:
  1.4 0.0 copy-start
  1.4 50.2 %shard_map.194 = f32[2,1,2048]{2,1,0:T(1,128)} custom-call(s32[2]{0:T(128)} %heights_in.1, s32[2]{0:T(128)} %widths_in.1, s32[2]{0:T(128)} %slot_in.1, f32[2,16,128]{2,1,0:T(8,128)} %bitcast.10, f32[5,16,1536]{2,1,0:T(8,128)} %bitcast.7, bf16[2,154,2,384]{3,2,1,0:T(2,128)(2,1)} %bitcast.8, bf16[64,1536]{1,0:T(8,128)(2,1)} %wp_in.1, ...), custom_call_target="tpu_custom_call" | custom-call | tf_op jit(solution)/shard_map/pallas_call | solution.py:637
  51.6 0.0 copy-done
  51.6 1.4 %multiply_subtract_fusion = (f32[2,1,2048]{2,1,0:T(1,128)}, f32[2,1,2048]{2,1,0:T(1,128)}) fusion(f32[2,1,2048]{2,1,0:T(1,128)S(1)} %copy-done, f32[2,1,2048]{2,1,0:T(1,128)} %shard_map.194, f32[]{:T(128)} %bitcast.1, f32[]{:T(128)S(6)} %sub.19), kind=kLoop, calls=%fused_computation | loop fusion | flops 16384 | bytes 65544 | tf_op jit(solution)/shard_map/sub | solution.py:709
Async XLA Ops:
  1.4 50.2 %copy-start = (f32[2,1,2048]{2,1,0:T(1,128)S(1)}, f32[2,1,2048]{2,1,0:T(1,128)}, u32[]{:S(2)}) copy-start(f32[2,1,2048]{2,1,0:T(1,128)} %param.19) | copy-start | bytes 49156

commit v5 on v4

--- a/solution.py
+++ b/solution.py
@@ -290,94 +290,6 @@
                 )
             )
             l_copies[-1].start()
-    for load in loads[3:]:
-        load.wait()
-    eb[...] = (lax.broadcasted_iota(jnp.int32, (480, 512), 1) == pick[...]).astype(F32).astype(BF16)
-    eo[...] = (lax.broadcasted_iota(jnp.int32, (144, 256), 1) == pick_o[...]).astype(F32).astype(BF16)
-
-    for copy in q_copies:
-        copy.wait_recv()
-    packed = jnp.dot(eb[...], qb[...].reshape(512, 128), preferred_element_type=F32).astype(BF16)
-    mine = core * 8 + by_c
-    for t in range(5):
-        qu[mine, :, t * 128 : (t + 1) * 128] = packed[t * 96 : (t + 1) * 96]
-
-    def unit(step):
-        return core * 8 + (by_c + step + 8) % 8
-
-    class Spread:
-        def __init__(self, buf, s_sem, r_sem, ps_sem, pr_sem):
-            self.buf, self.s, self.r, self.ps, self.pr = buf, s_sem, r_sem, ps_sem, pr_sem
-            self.cut = buf.shape[1] // 32 * 16 + buf.shape[1] % 32
-            self.sent, self.come = [], {}
-            self.partner = []
-
-        def send(self, n, origin, step, part=slice(None)):
-            ty, tz = ring_c((step + 8) % 8)
-            block = self.buf.at[unit(origin), part]
-            c = remote(
-                block,
-                block,
-                self.s.at[n],
-                self.r.at[n],
-                device(ty, tz, xh, core, xl),
-            )
-            c.start()
-            self.sent.append(c)
-            self.come[n] = c
-
-        def share(self, n, origin):
-            slot = unit(origin)
-            c = remote(
-                self.buf.at[slot],
-                self.buf.at[slot],
-                self.ps.at[n],
-                self.pr.at[n],
-                device(y, z, xh, 1 - core, xl),
-            )
-            c.start()
-            self.partner.append(c)
-
-        def first(self):
-            self.send(0, 0, 2)
-            self.send(1, 0, -2)
-            self.send(2, 0, 1)
-            self.send(3, 0, -1)
-            self.share(0, 0)
-
-        def second(self):
-            self.come[0].wait_recv()
-            self.send(4, -2, 1)
-            self.send(6, -2, 2, slice(0, self.cut))
-            self.come[1].wait_recv()
-            self.send(5, 2, -1)
-            self.send(7, 2, -2, slice(self.cut, None))
-            self.share(1, -2)
-            self.share(2, 2)
-            self.come[2].wait_recv()
-            self.share(3, -1)
-            self.come[3].wait_recv()
-            self.share(4, 1)
-
-        def third(self):
-            self.come[4].wait_recv()
-            self.share(5, -3)
-            self.come[5].wait_recv()
-            self.share(6, 3)
-            self.come[6].wait_recv()
-            self.come[7].wait_recv()
-            self.share(7, -4)
-
-        def last(self):
-            for c in self.partner:
-                c.wait_recv()
-
-        def close(self):
-            for c in self.sent + self.partner:
-                c.wait_send()
-
-    qs = Spread(qu, sem_us, sem_ur, sem_ps, sem_pr)
-    qs.first()
     for k in range(8):
         for dxh in range(2):
             for dxl in range(2):
@@ -397,6 +309,94 @@
                 o_copies[-1].start()
 
 
+    for load in loads[3:]:
+        load.wait()
+    eb[...] = (lax.broadcasted_iota(jnp.int32, (480, 512), 1) == pick[...]).astype(F32).astype(BF16)
+    eo[...] = (lax.broadcasted_iota(jnp.int32, (144, 256), 1) == pick_o[...]).astype(F32).astype(BF16)
+
+    for copy in q_copies:
+        copy.wait_recv()
+    packed = jnp.dot(eb[...], qb[...].reshape(512, 128), preferred_element_type=F32).astype(BF16)
+    mine = core * 8 + by_c
+    for t in range(5):
+        qu[mine, :, t * 128 : (t + 1) * 128] = packed[t * 96 : (t + 1) * 96]
+
+    def unit(step):
+        return core * 8 + (by_c + step + 8) % 8
+
+    class Spread:
+        def __init__(self, buf, s_sem, r_sem, ps_sem, pr_sem):
+            self.buf, self.s, self.r, self.ps, self.pr = buf, s_sem, r_sem, ps_sem, pr_sem
+            self.cut = buf.shape[1] // 32 * 16 + buf.shape[1] % 32
+            self.sent, self.come = [], {}
+            self.partner = []
+
+        def send(self, n, origin, step, part=slice(None)):
+            ty, tz = ring_c((step + 8) % 8)
+            block = self.buf.at[unit(origin), part]
+            c = remote(
+                block,
+                block,
+                self.s.at[n],
+                self.r.at[n],
+                device(ty, tz, xh, core, xl),
+            )
+            c.start()
+            self.sent.append(c)
+            self.come[n] = c
+
+        def share(self, n, origin):
+            slot = unit(origin)
+            c = remote(
+                self.buf.at[slot],
+                self.buf.at[slot],
+                self.ps.at[n],
+                self.pr.at[n],
+                device(y, z, xh, 1 - core, xl),
+            )
+            c.start()
+            self.partner.append(c)
+
+        def first(self):
+            self.send(0, 0, 2)
+            self.send(1, 0, -2)
+            self.send(2, 0, 1)
+            self.send(3, 0, -1)
+            self.share(0, 0)
+
+        def second(self):
+            self.come[0].wait_recv()
+            self.send(4, -2, 1)
+            self.send(6, -2, 2, slice(0, self.cut))
+            self.come[1].wait_recv()
+            self.send(5, 2, -1)
+            self.send(7, 2, -2, slice(self.cut, None))
+            self.share(1, -2)
+            self.share(2, 2)
+            self.come[2].wait_recv()
+            self.share(3, -1)
+            self.come[3].wait_recv()
+            self.share(4, 1)
+
+        def third(self):
+            self.come[4].wait_recv()
+            self.share(5, -3)
+            self.come[5].wait_recv()
+            self.share(6, 3)
+            self.come[6].wait_recv()
+            self.come[7].wait_recv()
+            self.share(7, -4)
+
+        def last(self):
+            for c in self.partner:
+                c.wait_recv()
+
+        def close(self):
+            for c in self.sent + self.partner:
+                c.wait_send()
+
+    qs = Spread(qu, sem_us, sem_ur, sem_ps, sem_pr)
+    qs.first()
     for copy in l_copies:
         copy.wait_recv()
     block = lb.at[pl.ds(pl.multiple_of(xh * 16, 16), 16)]
@@ -452,7 +452,9 @@
     c_id = lax.broadcasted_iota(jnp.int32, (384, 384), 1)
     pick_key = ((r_id == c_id + 192 * xh) & (c_id < 192)).astype(F32).astype(BF16)
     pick_val = ((r_id == c_id - 192 + 192 * xh) & (c_id >= 192)).astype(F32).astype(BF16)
-    place = ((r_id - 64 + 192 * xh == c_id) & (r_id >= 64)).astype(F32).astype(BF16)[0:256]
+    place = [
+        ((r_id - 64 + 192 * g == c_id) & (r_id >= 64)).astype(F32).astype(BF16)[0:256] for g in range(2)
+    ]
     text_rows = (
         jnp.dot(text[:, 0], pick_key, preferred_element_type=F32)
         + jnp.dot(text[:, 1], pick_val, preferred_element_type=F32)
@@ -531,7 +533,7 @@
     for h in range(3):
         inside = (lane >= 64 + 64 * h) & (lane < 128 + 64 * h)
         attended = attended + jnp.where(inside, acc[h * 128 : (h + 1) * 128], 0.0)
-    placed = jnp.dot(attended.astype(BF16), place, preferred_element_type=F32).astype(BF16)
+    placed = attended.astype(BF16)
     for j in range(4):
         for parity in range(2):
             send_att[j, parity * 16 : parity * 16 + 16] = placed[
@@ -557,9 +559,15 @@
     for copy in a_copies:
         copy.wait_recv()
 
-    halves = [
-        jnp.concatenate([recv_att[s, 2 * g] + recv_att[s, 2 * g + 1] for s in range(2)], 0) for g in range(2)
-    ]
+    halves = []
+    for g in range(2):
+        sides = [jnp.concatenate([recv_att[s, 2 * g + side] for s in range(2)], 0) for side in range(2)]
+        halves.append(
+            (
+                jnp.dot(sides[0], place[0], preferred_element_type=F32)
+                + jnp.dot(sides[1], place[1], preferred_element_type=F32)
+            ).astype(BF16)
+        )
     projected = lax.dot_general(
         jnp.concatenate(halves, 1), ou[...].reshape(D // 2, 768), nt, preferred_element_type=F32
     )
@@ -681,8 +689,8 @@
             pltpu.VMEM((176, D // 2), F32),
             pltpu.VMEM((480, 512), BF16),
             pltpu.VMEM((144, 256), BF16),
-            pltpu.VMEM((4, 32, 384), BF16),
-            pltpu.VMEM((2, 4, 32, 384), BF16),
+            pltpu.VMEM((4, 32, 256), BF16),
+            pltpu.VMEM((2, 4, 32, 256), BF16),
             pltpu.VMEM((3, 16, 128), F32),
             pltpu.VMEM((3, 16, 128), F32),
         ]

time: 53.4 us -> 53.3 us (level)
  no operation moved by 1% of the time
where the time goes in v5:
time: 53.3 us; the launch traced here: 53 us
  Pallas kernels  50.3 us (94%)
  between operations  1.4 us (3%)
  other arithmetic  1.36 us (3%)
    pallas_call x1, Pallas kernels, body(): pl.pallas_call(kernel, out_shape=shape, in_specs=[pl.BlockSpec(memory_spa...  50.3 us
    sub x1, other arithmetic, body(): latents - sigma_now * velocity  1.36 us

profile of v5, /device:TPU:1, one launch (start us, length us, event | category | flops | bytes accessed | tf_op | source)
XLA Modules:
  0.0 53.0 jit_solution(16052935130028064817)
XLA Ops:
  1.4 0.0 copy-start
  1.4 50.3 %shard_map.194 = f32[2,1,2048]{2,1,0:T(1,128)} custom-call(s32[2]{0:T(128)} %heights_in.1, s32[2]{0:T(128)} %widths_in.1, s32[2]{0:T(128)} %slot_in.1, f32[2,16,128]{2,1,0:T(8,128)} %bitcast.10, f32[5,16,1536]{2,1,0:T(8,128)} %bitcast.7, bf16[2,154,2,384]{3,2,1,0:T(2,128)(2,1)} %bitcast.8, bf16[64,1536]{1,0:T(8,128)(2,1)} %wp_in.1, ...), custom_call_target="tpu_custom_call" | custom-call | tf_op jit(solution)/shard_map/pallas_call | solution.py:645
  51.7 0.0 copy-done
  51.7 1.4 %multiply_subtract_fusion = (f32[2,1,2048]{2,1,0:T(1,128)}, f32[2,1,2048]{2,1,0:T(1,128)}) fusion(f32[2,1,2048]{2,1,0:T(1,128)S(1)} %copy-done, f32[2,1,2048]{2,1,0:T(1,128)} %shard_map.194, f32[]{:T(128)} %bitcast.1, f32[]{:T(128)S(6)} %sub.19), kind=kLoop, calls=%fused_computation | loop fusion | flops 16384 | bytes 65544 | tf_op jit(solution)/shard_map/sub | solution.py:717
Async XLA Ops:
  1.4 50.3 %copy-start = (f32[2,1,2048]{2,1,0:T(1,128)S(1)}, f32[2,1,2048]{2,1,0:T(1,128)}, u32[]{:S(2)}) copy-start(f32[2,1,2048]{2,1,0:T(1,128)} %param.19) | copy-start | bytes 49156

commit v6 on v5

--- a/solution.py
+++ b/solution.py
@@ -366,11 +366,11 @@
 
         def second(self):
             self.come[0].wait_recv()
+            self.send(6, -2, 2, slice(0, self.cut))
             self.send(4, -2, 1)
-            self.send(6, -2, 2, slice(0, self.cut))
             self.come[1].wait_recv()
+            self.send(7, 2, -2, slice(self.cut, None))
             self.send(5, 2, -1)
-            self.send(7, 2, -2, slice(self.cut, None))
             self.share(1, -2)
             self.share(2, 2)
             self.come[2].wait_recv()

time: 53.3 us -> 51.8 us (0.972)
  Pallas kernels: 50.3 us -> 48.8 us
    pallas_call x1, Pallas kernels: 50.3 us -> 48.8 us  [body(): pl.pallas_call(kernel, out_shape=shape, in_specs=[pl.BlockSpec(memory_spa...]
where the time goes in v6:
time: 51.8 us; the launch traced here: 51.6 us
  Pallas kernels  48.8 us (94%)
  between operations  1.4 us (3%)
  other arithmetic  1.36 us (3%)
    pallas_call x1, Pallas kernels, body(): pl.pallas_call(kernel, out_shape=shape, in_specs=[pl.BlockSpec(memory_spa...  48.8 us
    sub x1, other arithmetic, body(): latents - sigma_now * velocity  1.36 us

profile of v6, /device:TPU:1, one launch (start us, length us, event | category | flops | bytes accessed | tf_op | source)
XLA Modules:
  0.0 51.6 jit_solution(18241098479508191469)
XLA Ops:
  1.4 0.0 copy-start
  1.4 48.8 %shard_map.194 = f32[2,1,2048]{2,1,0:T(1,128)} custom-call(s32[2]{0:T(128)} %heights_in.1, s32[2]{0:T(128)} %widths_in.1, s32[2]{0:T(128)} %slot_in.1, f32[2,16,128]{2,1,0:T(8,128)} %bitcast.10, f32[5,16,1536]{2,1,0:T(8,128)} %bitcast.7, bf16[2,154,2,384]{3,2,1,0:T(2,128)(2,1)} %bitcast.8, bf16[64,1536]{1,0:T(8,128)(2,1)} %wp_in.1, ...), custom_call_target="tpu_custom_call" | custom-call | tf_op jit(solution)/shard_map/pallas_call | solution.py:645
  50.2 0.0 copy-done
  50.2 1.4 %multiply_subtract_fusion = (f32[2,1,2048]{2,1,0:T(1,128)}, f32[2,1,2048]{2,1,0:T(1,128)}) fusion(f32[2,1,2048]{2,1,0:T(1,128)S(1)} %copy-done, f32[2,1,2048]{2,1,0:T(1,128)} %shard_map.194, f32[]{:T(128)} %bitcast.1, f32[]{:T(128)S(6)} %sub.19), kind=kLoop, calls=%fused_computation | loop fusion | flops 16384 | bytes 65544 | tf_op jit(solution)/shard_map/sub | solution.py:717
Async XLA Ops:
  1.4 48.9 %copy-start = (f32[2,1,2048]{2,1,0:T(1,128)S(1)}, f32[2,1,2048]{2,1,0:T(1,128)}, u32[]{:S(2)}) copy-start(f32[2,1,2048]{2,1,0:T(1,128)} %param.19) | copy-start | bytes 49156
